TPU v7x, 256 devices: a whole 4x4x8 slice. The times are simulated.
256 devices in a mesh: ga: 4 (over z_hi), orb: 64 (over x, z_lo, y, core).
Axes of the slice: x: 4, y: 4, z: 8 (z_hi: 4, z_lo: 2; z = z_hi * 2 + z_lo), core: 2. Of those that a mesh axis runs over, the one named last changes fastest.
Arguments:
- coefficients: bfloat16 [2, 294912, 512], P(None, ('ga', 'orb')), may hold values from -0.01171875 to 0.01171875
- triples: int32 [3, 294912], P(None, ('ga', 'orb')), may hold values from -33 to 33
- elec_pos: float32 [3, 256], P(None, ('ga', 'orb')), may hold values from 0 to 1
- ion_pos: float32 [3, 128], replicated, may hold values from 0 to 1
- assignment: int32 [256], P(('ga', 'orb')), may hold values from 0 to 127
- rotation: int32 [256], P(('ga', 'orb')), may hold values from 0 to 63
- quad_table: float32 [64, 3, 12], replicated, may hold values from -2.4 to 2.4
- inverse_rows: float32 [256, 512], P(('ga', 'orb')), may hold values from -0.25 to 0.25
Outputs:
- ratios: float32 [256, 12], P(('ga', 'orb'))
All inputs are finite; a program needn't handle non-finite values.
Results may differ from a plain program's by a relative error of at most 0.0024.
Values may be sent and summed in bfloat16 or wider, within the bound.
No kernel may reach another device: no remote copies, remote signals or barrier semaphores. Data moves between devices by JAX's collectives and lax.ppermute only.
A program may use at most 64 MiB of HBM per device.

v0:
```python
import math

import jax
import jax.numpy as jnp
from jax import lax
from jax.sharding import PartitionSpec as P

TWO_PI = 2.0 * math.pi


def point_coords(elec_pos, ion_pos, assignment, rotation, quad_table):
    ion_rows = jnp.take(ion_pos, assignment, axis=1)
    offsets = elec_pos - ion_rows
    radius = jnp.sqrt(jnp.sum(offsets * offsets, axis=0))
    displace = jnp.take(quad_table, rotation, axis=0)
    located = ion_rows.T[:, :, None] + radius[:, None, None] * displace
    return jnp.transpose(located, (1, 0, 2)).reshape(3, -1)


def phase_values(points, triples, coefficients):
    point_count = points.shape[1]
    wave_count = triples.shape[1]
    columns = coefficients.shape[2]
    block_rows = math.gcd(point_count, 512)
    waves = triples.astype(jnp.float32) * TWO_PI

    def one_block(block_points):

        def add_panel(step_index, running):
            angle = (
                block_points[0][:, None] * waves[0][None, :]
                + block_points[1][:, None] * waves[1][None, :]
                + block_points[2][:, None] * waves[2][None, :]
            )
            phases = jnp.concatenate(
                [jnp.cos(angle).astype(jnp.bfloat16), jnp.sin(angle).astype(jnp.bfloat16)], axis=1
            )
            weights = coefficients.reshape(2 * wave_count, columns)
            return running + jnp.dot(phases, weights, preferred_element_type=jnp.float32)

        initial = jnp.zeros((block_rows, columns), jnp.float32)
        return lax.fori_loop(0, wave_count // wave_count, add_panel, initial)

    blocks = jnp.transpose(points.reshape(3, point_count // block_rows, block_rows), (1, 0, 2))
    return lax.map(one_block, blocks).reshape(point_count, columns)


def on_device(
    coefficients, triples, elec_pos, ion_pos, assignment, rotation, quad_table, inverse_rows
):
    local_points = point_coords(elec_pos, ion_pos, assignment, rotation, quad_table)
    all_points = lax.all_gather(local_points, ("ga", "orb"), axis=1, tiled=True)
    electrons = inverse_rows.shape[0]
    values = lax.psum_scatter(
        phase_values(all_points, triples, coefficients),
        ("ga", "orb"),
        scatter_dimension=0,
        tiled=True,
    )
    shaped = values.reshape(electrons, values.shape[0] // electrons, values.shape[1])
    return jnp.sum(shaped * inverse_rows[:, None, :], axis=2)


def solution(mesh):
    return jax.shard_map(
        on_device,
        mesh=mesh,
        in_specs=(
            P(None, ("ga", "orb"), None),
            P(None, ("ga", "orb")),
            P(None, ("ga", "orb")),
            P(),
            P(("ga", "orb")),
            P(("ga", "orb")),
            P(),
            P(("ga", "orb"), None),
        ),
        out_specs=P(("ga", "orb"), None),
        check_vma=False,
    )
```

profile of v0, /device:TPU:1, one launch (start us, length us, event | category | flops | bytes accessed | tf_op | source)
XLA Modules:
  0.0 1625.1 jit_solution(16454387211662428138)
XLA Ops:
  5.1 351.9 %all-gather = f32[256,12,3]{1,2,0:T(4,128)S(1)} all-gather(f32[1,12,3]{1,2,0:T(4,128)S(1)} %add_bitcast_fusion), channel_id=1, replica_groups=mesh['ga'=4,'orb'=64] {'ga','orb'}, dimensions={0}, use_global_device_ids=true | all-gather | bytes 37008 | tf_op jit(solution)/shard_map/all_gather | solution.py:52
  358.1 70.7 %while.16 = (s32[]{:T(128)}, f32[6,512,512]{2,1,0:T(8,128)}, f32[6,3,512]{2,0,1:T(8,128)S(1)}, f32[3,1152]{1,0:T(4,128)S(1)}, bf16[2,1152,512]{2,1,0:T(8,128)(2,1)}, /*index=5*/s32[]{:T(128)}, s32[]{:T(128)}, s32[]{}, s32[]{}) while((s32[]{:T(128)}, f32[6,512,512]{2,1,0:T(8,128)}, f32[6,3,512]{2,0,1:T(8,128)S(1)}, f32[3,1152]{1,0:T(4,128)S(1)}, ...), condition=%wide.region_2.3_spmd, body=%wide.region_1.2_spmd.sunk | while | flops 1216806912 | bytes 17624220 | solution.py:45
  358.2 9.3 cosine_convert_fusion.2
  370.0 9.3 cosine_convert_fusion.2
  381.8 9.3 cosine_convert_fusion.2
  393.5 9.3 cosine_convert_fusion.2
  405.3 9.3 cosine_convert_fusion.2
  417.1 9.3 cosine_convert_fusion.2
  428.8 682.5 %fusion = f32[16,512]{1,0:T(8,128)S(1)} fusion(f32[3072,512]{1,0:T(8,128)} %bitcast.42), kind=kCustom, calls=%all-reduce-scatter | all-reduce-scatter fusion | flops 2097153 | bytes 6324224
  1111.3 7.0 collective-permute-start
  1118.4 13.1 collective-permute-start.1
  1131.5 13.1 collective-permute-start.10
  1144.7 4.6 collective-permute-start.63
  1149.2 11.6 collective-permute-start.11
  1160.8 13.1 collective-permute-start.12
  1174.0 13.1 collective-permute-start.13
  1187.1 13.1 collective-permute-start.14
  1200.2 13.1 collective-permute-start.15
  1213.4 13.1 collective-permute-start.16
  1226.5 13.1 collective-permute-start.17
  1239.7 13.1 collective-permute-start.18
  1252.8 13.1 collective-permute-start.19
  1265.9 13.1 collective-permute-start.2
  1279.1 13.1 collective-permute-start.20
  1292.2 13.1 collective-permute-start.21
  1305.4 13.1 collective-permute-start.22
  1318.5 13.1 collective-permute-start.23
  1331.6 13.1 collective-permute-start.24
  1344.8 13.1 collective-permute-start.25
  1357.9 13.1 collective-permute-start.26
  1371.1 13.1 collective-permute-start.27
  1384.2 13.1 collective-permute-start.28
  1397.3 6.6 collective-permute-start.29
  1404.0 10.1 collective-permute-start.3
  1414.1 5.0 collective-permute-start.30
  1419.2 4.4 collective-permute-start.31
  1423.6 5.8 collective-permute-start.32
  1429.4 6.7 collective-permute-start.33
  1436.1 6.2 collective-permute-start.34
  1442.3 4.7 collective-permute-start.35
  1447.0 6.8 collective-permute-start.36
  1455.2 4.1 collective-permute-start.38
  1460.7 3.1 collective-permute-start.4
  1463.7 7.1 collective-permute-start.40
  1470.8 4.3 collective-permute-start.41
  1475.2 6.5 collective-permute-start.42
  1481.6 5.9 collective-permute-start.43
  1487.5 4.1 collective-permute-start.44
  1491.7 3.2 collective-permute-start.45
  1495.0 3.2 collective-permute-start.46
  1503.1 5.3 collective-permute-start.5
  1508.4 7.2 collective-permute-start.50
  1515.6 5.8 collective-permute-start.51
  1521.5 6.8 collective-permute-start.52
  1530.6 3.0 collective-permute-start.54
  1539.1 3.5 collective-permute-start.58
  1544.3 5.5 collective-permute-start.6
  1549.8 8.1 collective-permute-start.60
  1558.0 4.8 collective-permute-start.61
  1562.8 5.7 collective-permute-start.62
  1568.5 4.4 collective-permute-start.7
  1572.9 13.1 collective-permute-start.8
  1586.0 13.7 collective-permute-start.9
  1601.2 23.3 %concatenate.6 = f32[1036,512]{1,0:T(8,128)S(1)} concatenate(f32[12,512]{1,0:T(8,128)S(1)} %collective-permute-done.63, f32[16,512]{1,0:T(8,128)} %copy-done.18, f32[16,512]{1,0:T(8,128)} %copy-done.17, f32[16,512]{1,0:T(8,128)} %copy-done.16, f32[16,512]{1,0:T(8,128)} %copy-done.14, f32[16,512]{1,0:T(8,128)} %copy-done.13, f32[16,512]{1,0:T(8,128)} %copy-done.12, ...), dimensions={0} | concatenate | bytes 4243456
  (159 shorter events, 37.8 us)
Async XLA Ops:
  1111.3 62.6 %collective-permute-start = (f32[16,512]{1,0:T(8,128)S(1)}, f32[16,512]{1,0:T(8,128)S(1)}, u32[]{:S(2)}, u32[]{:S(2)}) collective-permute-start(f32[16,512]{1,0:T(8,128)S(1)} %fusion), channel_id=1, source_target_pairs={{0,1},{1,2},{2,3},{3,4},{4,5},{5,6},{6,7},{7,8},{8,9},{9,10},{10,1... | collective-permute-start | bytes 98312
  1118.4 68.7 %collective-permute-start.1 = (f32[16,512]{1,0:T(8,128)S(1)}, f32[16,512]{1,0:T(8,128)S(1)}, u32[]{:S(2)}, u32[]{:S(2)}) collective-permute-start(f32[16,512]{1,0:T(8,128)S(1)} %fusion), channel_id=1, source_target_pairs={{0,2},{1,3},{2,4},{3,5},{4,6},{5,7},{6,8},{7,9},{8,10},{9,11},{10,... | collective-permute-start | bytes 98312
  1131.5 68.7 %collective-permute-start.10 = (f32[16,512]{1,0:T(8,128)S(1)}, f32[16,512]{1,0:T(8,128)S(1)}, u32[]{:S(2)}, u32[]{:S(2)}) collective-permute-start(f32[16,512]{1,0:T(8,128)S(1)} %fusion), channel_id=1, source_target_pairs={{0,11},{1,12},{2,13},{3,14},{4,15},{5,16},{6,17},{7,18},{8,19},{9,... | collective-permute-start | bytes 98312
  1144.7 16.2 collective-permute-start.63
  1149.2 64.1 %collective-permute-start.11 = (f32[16,512]{1,0:T(8,128)S(1)}, f32[16,512]{1,0:T(8,128)S(1)}, u32[]{:S(2)}, u32[]{:S(2)}) collective-permute-start(f32[16,512]{1,0:T(8,128)S(1)} %fusion), channel_id=1, source_target_pairs={{0,12},{1,13},{2,14},{3,15},{4,16},{5,17},{6,18},{7,19},{8,20},{9,... | collective-permute-start | bytes 98312
  1160.8 65.7 %collective-permute-start.12 = (f32[16,512]{1,0:T(8,128)S(1)}, f32[16,512]{1,0:T(8,128)S(1)}, u32[]{:S(2)}, u32[]{:S(2)}) collective-permute-start(f32[16,512]{1,0:T(8,128)S(1)} %fusion), channel_id=1, source_target_pairs={{0,13},{1,14},{2,15},{3,16},{4,17},{5,18},{6,19},{7,20},{8,21},{9,... | collective-permute-start | bytes 98312
  1174.0 65.7 %collective-permute-start.13 = (f32[16,512]{1,0:T(8,128)S(1)}, f32[16,512]{1,0:T(8,128)S(1)}, u32[]{:S(2)}, u32[]{:S(2)}) collective-permute-start(f32[16,512]{1,0:T(8,128)S(1)} %fusion), channel_id=1, source_target_pairs={{0,14},{1,15},{2,16},{3,17},{4,18},{5,19},{6,20},{7,21},{8,22},{9,... | collective-permute-start | bytes 98312
  1187.1 65.7 %collective-permute-start.14 = (f32[16,512]{1,0:T(8,128)S(1)}, f32[16,512]{1,0:T(8,128)S(1)}, u32[]{:S(2)}, u32[]{:S(2)}) collective-permute-start(f32[16,512]{1,0:T(8,128)S(1)} %fusion), channel_id=1, source_target_pairs={{0,15},{1,16},{2,17},{3,18},{4,19},{5,20},{6,21},{7,22},{8,23},{9,... | collective-permute-start | bytes 98312
  1200.2 65.7 %collective-permute-start.15 = (f32[16,512]{1,0:T(8,128)S(1)}, f32[16,512]{1,0:T(8,128)S(1)}, u32[]{:S(2)}, u32[]{:S(2)}) collective-permute-start(f32[16,512]{1,0:T(8,128)S(1)} %fusion), channel_id=1, source_target_pairs={{0,16},{1,17},{2,18},{3,19},{4,20},{5,21},{6,22},{7,23},{8,24},{9,... | collective-permute-start | bytes 98312
  1213.4 65.7 %collective-permute-start.16 = (f32[16,512]{1,0:T(8,128)S(1)}, f32[16,512]{1,0:T(8,128)S(1)}, u32[]{:S(2)}, u32[]{:S(2)}) collective-permute-start(f32[16,512]{1,0:T(8,128)S(1)} %fusion), channel_id=1, source_target_pairs={{0,17},{1,18},{2,19},{3,20},{4,21},{5,22},{6,23},{7,24},{8,25},{9,... | collective-permute-start | bytes 98312
  1226.5 65.7 %collective-permute-start.17 = (f32[16,512]{1,0:T(8,128)S(1)}, f32[16,512]{1,0:T(8,128)S(1)}, u32[]{:S(2)}, u32[]{:S(2)}) collective-permute-start(f32[16,512]{1,0:T(8,128)S(1)} %fusion), channel_id=1, source_target_pairs={{0,18},{1,19},{2,20},{3,21},{4,22},{5,23},{6,24},{7,25},{8,26},{9,... | collective-permute-start | bytes 98312
  1239.7 65.7 %collective-permute-start.18 = (f32[16,512]{1,0:T(8,128)S(1)}, f32[16,512]{1,0:T(8,128)S(1)}, u32[]{:S(2)}, u32[]{:S(2)}) collective-permute-start(f32[16,512]{1,0:T(8,128)S(1)} %fusion), channel_id=1, source_target_pairs={{0,19},{1,20},{2,21},{3,22},{4,23},{5,24},{6,25},{7,26},{8,27},{9,... | collective-permute-start | bytes 98312
  1252.8 65.7 %collective-permute-start.19 = (f32[16,512]{1,0:T(8,128)S(1)}, f32[16,512]{1,0:T(8,128)S(1)}, u32[]{:S(2)}, u32[]{:S(2)}) collective-permute-start(f32[16,512]{1,0:T(8,128)S(1)} %fusion), channel_id=1, source_target_pairs={{0,20},{1,21},{2,22},{3,23},{4,24},{5,25},{6,26},{7,27},{8,28},{9,... | collective-permute-start | bytes 98312
  1265.9 65.7 %collective-permute-start.2 = (f32[16,512]{1,0:T(8,128)S(1)}, f32[16,512]{1,0:T(8,128)S(1)}, u32[]{:S(2)}, u32[]{:S(2)}) collective-permute-start(f32[16,512]{1,0:T(8,128)S(1)} %fusion), channel_id=1, source_target_pairs={{0,3},{1,4},{2,5},{3,6},{4,7},{5,8},{6,9},{7,10},{8,11},{9,12},{10... | collective-permute-start | bytes 98312
  1279.1 65.7 %collective-permute-start.20 = (f32[16,512]{1,0:T(8,128)S(1)}, f32[16,512]{1,0:T(8,128)S(1)}, u32[]{:S(2)}, u32[]{:S(2)}) collective-permute-start(f32[16,512]{1,0:T(8,128)S(1)} %fusion), channel_id=1, source_target_pairs={{0,21},{1,22},{2,23},{3,24},{4,25},{5,26},{6,27},{7,28},{8,29},{9,... | collective-permute-start | bytes 98312
  1292.2 65.7 %collective-permute-start.21 = (f32[16,512]{1,0:T(8,128)S(1)}, f32[16,512]{1,0:T(8,128)S(1)}, u32[]{:S(2)}, u32[]{:S(2)}) collective-permute-start(f32[16,512]{1,0:T(8,128)S(1)} %fusion), channel_id=1, source_target_pairs={{0,22},{1,23},{2,24},{3,25},{4,26},{5,27},{6,28},{7,29},{8,30},{9,... | collective-permute-start | bytes 98312
  1305.4 65.7 %collective-permute-start.22 = (f32[16,512]{1,0:T(8,128)S(1)}, f32[16,512]{1,0:T(8,128)S(1)}, u32[]{:S(2)}, u32[]{:S(2)}) collective-permute-start(f32[16,512]{1,0:T(8,128)S(1)} %fusion), channel_id=1, source_target_pairs={{0,23},{1,24},{2,25},{3,26},{4,27},{5,28},{6,29},{7,30},{8,31},{9,... | collective-permute-start | bytes 98312
  1318.5 65.7 %collective-permute-start.23 = (f32[16,512]{1,0:T(8,128)S(1)}, f32[16,512]{1,0:T(8,128)S(1)}, u32[]{:S(2)}, u32[]{:S(2)}) collective-permute-start(f32[16,512]{1,0:T(8,128)S(1)} %fusion), channel_id=1, source_target_pairs={{0,24},{1,25},{2,26},{3,27},{4,28},{5,29},{6,30},{7,31},{8,32},{9,... | collective-permute-start | bytes 98312
  1331.6 65.7 %collective-permute-start.24 = (f32[16,512]{1,0:T(8,128)S(1)}, f32[16,512]{1,0:T(8,128)S(1)}, u32[]{:S(2)}, u32[]{:S(2)}) collective-permute-start(f32[16,512]{1,0:T(8,128)S(1)} %fusion), channel_id=1, source_target_pairs={{0,25},{1,26},{2,27},{3,28},{4,29},{5,30},{6,31},{7,32},{8,33},{9,... | collective-permute-start | bytes 98312
  1344.8 59.2 %collective-permute-start.25 = (f32[16,512]{1,0:T(8,128)S(1)}, f32[16,512]{1,0:T(8,128)S(1)}, u32[]{:S(2)}, u32[]{:S(2)}) collective-permute-start(f32[16,512]{1,0:T(8,128)S(1)} %fusion), channel_id=1, source_target_pairs={{0,26},{1,27},{2,28},{3,29},{4,30},{5,31},{6,32},{7,33},{8,34},{9,... | collective-permute-start | bytes 98312
  1357.9 56.2 %collective-permute-start.26 = (f32[16,512]{1,0:T(8,128)S(1)}, f32[16,512]{1,0:T(8,128)S(1)}, u32[]{:S(2)}, u32[]{:S(2)}) collective-permute-start(f32[16,512]{1,0:T(8,128)S(1)} %fusion), channel_id=1, source_target_pairs={{0,27},{1,28},{2,29},{3,30},{4,31},{5,32},{6,33},{7,34},{8,35},{9,... | collective-permute-start | bytes 98312
  1371.1 48.1 %collective-permute-start.27 = (f32[16,512]{1,0:T(8,128)S(1)}, f32[16,512]{1,0:T(8,128)S(1)}, u32[]{:S(2)}, u32[]{:S(2)}) collective-permute-start(f32[16,512]{1,0:T(8,128)S(1)} %fusion), channel_id=1, source_target_pairs={{0,28},{1,29},{2,30},{3,31},{4,32},{5,33},{6,34},{7,35},{8,36},{9,... | collective-permute-start | bytes 98312
  1384.2 39.4 %collective-permute-start.28 = (f32[16,512]{1,0:T(8,128)S(1)}, f32[16,512]{1,0:T(8,128)S(1)}, u32[]{:S(2)}, u32[]{:S(2)}) collective-permute-start(f32[16,512]{1,0:T(8,128)S(1)} %fusion), channel_id=1, source_target_pairs={{0,29},{1,30},{2,31},{3,32},{4,33},{5,34},{6,35},{7,36},{8,37},{9,... | collective-permute-start | bytes 98312
  1397.3 32.0 %collective-permute-start.29 = (f32[16,512]{1,0:T(8,128)S(1)}, f32[16,512]{1,0:T(8,128)S(1)}, u32[]{:S(2)}, u32[]{:S(2)}) collective-permute-start(f32[16,512]{1,0:T(8,128)S(1)} %fusion), channel_id=1, source_target_pairs={{0,30},{1,31},{2,32},{3,33},{4,34},{5,35},{6,36},{7,37},{8,38},{9,... | collective-permute-start | bytes 98312
  1404.0 32.1 %collective-permute-start.3 = (f32[16,512]{1,0:T(8,128)S(1)}, f32[16,512]{1,0:T(8,128)S(1)}, u32[]{:S(2)}, u32[]{:S(2)}) collective-permute-start(f32[16,512]{1,0:T(8,128)S(1)} %fusion), channel_id=1, source_target_pairs={{0,4},{1,5},{2,6},{3,7},{4,8},{5,9},{6,10},{7,11},{8,12},{9,13},{1... | collective-permute-start | bytes 98312
  1414.1 28.2 %collective-permute-start.30 = (f32[16,512]{1,0:T(8,128)S(1)}, f32[16,512]{1,0:T(8,128)S(1)}, u32[]{:S(2)}, u32[]{:S(2)}) collective-permute-start(f32[16,512]{1,0:T(8,128)S(1)} %fusion), channel_id=1, source_target_pairs={{0,31},{1,32},{2,33},{3,34},{4,35},{5,36},{6,37},{7,38},{8,39},{9,... | collective-permute-start | bytes 98312
  1419.2 27.9 %collective-permute-start.31 = (f32[16,512]{1,0:T(8,128)S(1)}, f32[16,512]{1,0:T(8,128)S(1)}, u32[]{:S(2)}, u32[]{:S(2)}) collective-permute-start(f32[16,512]{1,0:T(8,128)S(1)} %fusion), channel_id=1, source_target_pairs={{0,32},{1,33},{2,34},{3,35},{4,36},{5,37},{6,38},{7,39},{8,40},{9,... | collective-permute-start | bytes 98312
  1423.6 30.3 %collective-permute-start.32 = (f32[16,512]{1,0:T(8,128)S(1)}, f32[16,512]{1,0:T(8,128)S(1)}, u32[]{:S(2)}, u32[]{:S(2)}) collective-permute-start(f32[16,512]{1,0:T(8,128)S(1)} %fusion), channel_id=1, source_target_pairs={{0,33},{1,34},{2,35},{3,36},{4,37},{5,38},{6,39},{7,40},{8,41},{9,... | collective-permute-start | bytes 98312
  1429.4 25.8 %collective-permute-start.33 = (f32[16,512]{1,0:T(8,128)S(1)}, f32[16,512]{1,0:T(8,128)S(1)}, u32[]{:S(2)}, u32[]{:S(2)}) collective-permute-start(f32[16,512]{1,0:T(8,128)S(1)} %fusion), channel_id=1, source_target_pairs={{0,34},{1,35},{2,36},{3,37},{4,38},{5,39},{6,40},{7,41},{8,42},{9,... | collective-permute-start | bytes 98312
  1436.1 23.2 %collective-permute-start.34 = (f32[16,512]{1,0:T(8,128)S(1)}, f32[16,512]{1,0:T(8,128)S(1)}, u32[]{:S(2)}, u32[]{:S(2)}) collective-permute-start(f32[16,512]{1,0:T(8,128)S(1)} %fusion), channel_id=1, source_target_pairs={{0,35},{1,36},{2,37},{3,38},{4,39},{5,40},{6,41},{7,42},{8,43},{9,... | collective-permute-start | bytes 98312
  1442.3 18.3 %collective-permute-start.35 = (f32[16,512]{1,0:T(8,128)S(1)}, f32[16,512]{1,0:T(8,128)S(1)}, u32[]{:S(2)}, u32[]{:S(2)}) collective-permute-start(f32[16,512]{1,0:T(8,128)S(1)} %fusion), channel_id=1, source_target_pairs={{0,36},{1,37},{2,38},{3,39},{4,40},{5,41},{6,42},{7,43},{8,44},{9,... | collective-permute-start | bytes 98312
  1447.0 16.7 %collective-permute-start.36 = (f32[16,512]{1,0:T(8,128)S(1)}, f32[16,512]{1,0:T(8,128)S(1)}, u32[]{:S(2)}, u32[]{:S(2)}) collective-permute-start(f32[16,512]{1,0:T(8,128)S(1)} %fusion), channel_id=1, source_target_pairs={{0,37},{1,38},{2,39},{3,40},{4,41},{5,42},{6,43},{7,44},{8,45},{9,... | collective-permute-start | bytes 98312
  1453.9 16.9 %collective-permute-start.37 = (f32[16,512]{1,0:T(8,128)S(1)}, f32[16,512]{1,0:T(8,128)S(1)}, u32[]{:S(2)}, u32[]{:S(2)}) collective-permute-start(f32[16,512]{1,0:T(8,128)S(1)} %fusion), channel_id=1, source_target_pairs={{0,38},{1,39},{2,40},{3,41},{4,42},{5,43},{6,44},{7,45},{8,46},{9,... | collective-permute-start | bytes 98312
  1455.2 20.0 %collective-permute-start.38 = (f32[16,512]{1,0:T(8,128)S(1)}, f32[16,512]{1,0:T(8,128)S(1)}, u32[]{:S(2)}, u32[]{:S(2)}) collective-permute-start(f32[16,512]{1,0:T(8,128)S(1)} %fusion), channel_id=1, source_target_pairs={{0,39},{1,40},{2,41},{3,42},{4,43},{5,44},{6,45},{7,46},{8,47},{9,... | collective-permute-start | bytes 98312
  1459.3 22.3 %collective-permute-start.39 = (f32[16,512]{1,0:T(8,128)S(1)}, f32[16,512]{1,0:T(8,128)S(1)}, u32[]{:S(2)}, u32[]{:S(2)}) collective-permute-start(f32[16,512]{1,0:T(8,128)S(1)} %fusion), channel_id=1, source_target_pairs={{0,40},{1,41},{2,42},{3,43},{4,44},{5,45},{6,46},{7,47},{8,48},{9,... | collective-permute-start | bytes 98312
  1460.7 26.9 %collective-permute-start.4 = (f32[16,512]{1,0:T(8,128)S(1)}, f32[16,512]{1,0:T(8,128)S(1)}, u32[]{:S(2)}, u32[]{:S(2)}) collective-permute-start(f32[16,512]{1,0:T(8,128)S(1)} %fusion), channel_id=1, source_target_pairs={{0,5},{1,6},{2,7},{3,8},{4,9},{5,10},{6,11},{7,12},{8,13},{9,14},{... | collective-permute-start | bytes 98312
  1463.7 27.9 %collective-permute-start.40 = (f32[16,512]{1,0:T(8,128)S(1)}, f32[16,512]{1,0:T(8,128)S(1)}, u32[]{:S(2)}, u32[]{:S(2)}) collective-permute-start(f32[16,512]{1,0:T(8,128)S(1)} %fusion), channel_id=1, source_target_pairs={{0,41},{1,42},{2,43},{3,44},{4,45},{5,46},{6,47},{7,48},{8,49},{9,... | collective-permute-start | bytes 98312
  1470.8 24.1 %collective-permute-start.41 = (f32[16,512]{1,0:T(8,128)S(1)}, f32[16,512]{1,0:T(8,128)S(1)}, u32[]{:S(2)}, u32[]{:S(2)}) collective-permute-start(f32[16,512]{1,0:T(8,128)S(1)} %fusion), channel_id=1, source_target_pairs={{0,42},{1,43},{2,44},{3,45},{4,46},{5,47},{6,48},{7,49},{8,50},{9,... | collective-permute-start | bytes 98312
  1475.2 23.0 %collective-permute-start.42 = (f32[16,512]{1,0:T(8,128)S(1)}, f32[16,512]{1,0:T(8,128)S(1)}, u32[]{:S(2)}, u32[]{:S(2)}) collective-permute-start(f32[16,512]{1,0:T(8,128)S(1)} %fusion), channel_id=1, source_target_pairs={{0,43},{1,44},{2,45},{3,46},{4,47},{5,48},{6,49},{7,50},{8,51},{9,... | collective-permute-start | bytes 98312
  1481.6 18.2 %collective-permute-start.43 = (f32[16,512]{1,0:T(8,128)S(1)}, f32[16,512]{1,0:T(8,128)S(1)}, u32[]{:S(2)}, u32[]{:S(2)}) collective-permute-start(f32[16,512]{1,0:T(8,128)S(1)} %fusion), channel_id=1, source_target_pairs={{0,44},{1,45},{2,46},{3,47},{4,48},{5,49},{6,50},{7,51},{8,52},{9,... | collective-permute-start | bytes 98312
  1487.5 14.2 collective-permute-start.44
  1491.7 11.4 collective-permute-start.45
  1495.0 13.4 collective-permute-start.46
  1498.2 17.5 %collective-permute-start.47 = (f32[16,512]{1,0:T(8,128)S(1)}, f32[16,512]{1,0:T(8,128)S(1)}, u32[]{:S(2)}, u32[]{:S(2)}) collective-permute-start(f32[16,512]{1,0:T(8,128)S(1)} %fusion), channel_id=1, source_target_pairs={{0,48},{1,49},{2,50},{3,51},{4,52},{5,53},{6,54},{7,55},{8,56},{9,... | collective-permute-start | bytes 98312
  1499.8 21.7 %collective-permute-start.48 = (f32[16,512]{1,0:T(8,128)S(1)}, f32[16,512]{1,0:T(8,128)S(1)}, u32[]{:S(2)}, u32[]{:S(2)}) collective-permute-start(f32[16,512]{1,0:T(8,128)S(1)} %fusion), channel_id=1, source_target_pairs={{0,49},{1,50},{2,51},{3,52},{4,53},{5,54},{6,55},{7,56},{8,57},{9,... | collective-permute-start | bytes 98312
  1501.8 26.5 %collective-permute-start.49 = (f32[16,512]{1,0:T(8,128)S(1)}, f32[16,512]{1,0:T(8,128)S(1)}, u32[]{:S(2)}, u32[]{:S(2)}) collective-permute-start(f32[16,512]{1,0:T(8,128)S(1)} %fusion), channel_id=1, source_target_pairs={{0,50},{1,51},{2,52},{3,53},{4,54},{5,55},{6,56},{7,57},{8,58},{9,... | collective-permute-start | bytes 98312
  1503.1 27.5 %collective-permute-start.5 = (f32[16,512]{1,0:T(8,128)S(1)}, f32[16,512]{1,0:T(8,128)S(1)}, u32[]{:S(2)}, u32[]{:S(2)}) collective-permute-start(f32[16,512]{1,0:T(8,128)S(1)} %fusion), channel_id=1, source_target_pairs={{0,6},{1,7},{2,8},{3,9},{4,10},{5,11},{6,12},{7,13},{8,14},{9,15},... | collective-permute-start | bytes 98312
  1508.4 25.2 %collective-permute-start.50 = (f32[16,512]{1,0:T(8,128)S(1)}, f32[16,512]{1,0:T(8,128)S(1)}, u32[]{:S(2)}, u32[]{:S(2)}) collective-permute-start(f32[16,512]{1,0:T(8,128)S(1)} %fusion), channel_id=1, source_target_pairs={{0,51},{1,52},{2,53},{3,54},{4,55},{5,56},{6,57},{7,58},{8,59},{9,... | collective-permute-start | bytes 98312
  1515.6 19.4 %collective-permute-start.51 = (f32[16,512]{1,0:T(8,128)S(1)}, f32[16,512]{1,0:T(8,128)S(1)}, u32[]{:S(2)}, u32[]{:S(2)}) collective-permute-start(f32[16,512]{1,0:T(8,128)S(1)} %fusion), channel_id=1, source_target_pairs={{0,52},{1,53},{2,54},{3,55},{4,56},{5,57},{6,58},{7,59},{8,60},{9,... | collective-permute-start | bytes 98312
  1521.5 16.1 collective-permute-start.52
  1528.3 10.8 collective-permute-start.53
  1530.6 12.0 collective-permute-start.54
  1533.7 10.6 collective-permute-start.55
  1535.0 14.7 collective-permute-start.56
  1537.6 20.4 %collective-permute-start.57 = (f32[16,512]{1,0:T(8,128)S(1)}, f32[16,512]{1,0:T(8,128)S(1)}, u32[]{:S(2)}, u32[]{:S(2)}) collective-permute-start(f32[16,512]{1,0:T(8,128)S(1)} %fusion), channel_id=1, source_target_pairs={{0,58},{1,59},{2,60},{3,61},{4,62},{5,63},{6,64},{7,65},{8,66},{9,... | collective-permute-start | bytes 98312
  1539.1 23.6 %collective-permute-start.58 = (f32[16,512]{1,0:T(8,128)S(1)}, f32[16,512]{1,0:T(8,128)S(1)}, u32[]{:S(2)}, u32[]{:S(2)}) collective-permute-start(f32[16,512]{1,0:T(8,128)S(1)} %fusion), channel_id=1, source_target_pairs={{0,59},{1,60},{2,61},{3,62},{4,63},{5,64},{6,65},{7,66},{8,67},{9,... | collective-permute-start | bytes 98312
  1542.6 25.8 %collective-permute-start.59 = (f32[16,512]{1,0:T(8,128)S(1)}, f32[16,512]{1,0:T(8,128)S(1)}, u32[]{:S(2)}, u32[]{:S(2)}) collective-permute-start(f32[16,512]{1,0:T(8,128)S(1)} %fusion), channel_id=1, source_target_pairs={{0,60},{1,61},{2,62},{3,63},{4,64},{5,65},{6,66},{7,67},{8,68},{9,... | collective-permute-start | bytes 98312
  1544.3 28.6 %collective-permute-start.6 = (f32[16,512]{1,0:T(8,128)S(1)}, f32[16,512]{1,0:T(8,128)S(1)}, u32[]{:S(2)}, u32[]{:S(2)}) collective-permute-start(f32[16,512]{1,0:T(8,128)S(1)} %fusion), channel_id=1, source_target_pairs={{0,7},{1,8},{2,9},{3,10},{4,11},{5,12},{6,13},{7,14},{8,15},{9,16}... | collective-permute-start | bytes 98312
  1549.8 36.2 %collective-permute-start.60 = (f32[16,512]{1,0:T(8,128)S(1)}, f32[16,512]{1,0:T(8,128)S(1)}, u32[]{:S(2)}, u32[]{:S(2)}) collective-permute-start(f32[16,512]{1,0:T(8,128)S(1)} %fusion), channel_id=1, source_target_pairs={{0,61},{1,62},{2,63},{3,64},{4,65},{5,66},{6,67},{7,68},{8,69},{9,... | collective-permute-start | bytes 98312
  1558.0 41.9 %collective-permute-start.61 = (f32[16,512]{1,0:T(8,128)S(1)}, f32[16,512]{1,0:T(8,128)S(1)}, u32[]{:S(2)}, u32[]{:S(2)}) collective-permute-start(f32[16,512]{1,0:T(8,128)S(1)} %fusion), channel_id=1, source_target_pairs={{0,62},{1,63},{2,64},{3,65},{4,66},{5,67},{6,68},{7,69},{8,70},{9,... | collective-permute-start | bytes 98312
  1562.8 37.2 %collective-permute-start.62 = (f32[16,512]{1,0:T(8,128)S(1)}, f32[16,512]{1,0:T(8,128)S(1)}, u32[]{:S(2)}, u32[]{:S(2)}) collective-permute-start(f32[16,512]{1,0:T(8,128)S(1)} %fusion), channel_id=1, source_target_pairs={{0,63},{1,64},{2,65},{3,66},{4,67},{5,68},{6,69},{7,70},{8,71},{9,... | collective-permute-start | bytes 98312
  1568.5 31.5 %collective-permute-start.7 = (f32[16,512]{1,0:T(8,128)S(1)}, f32[16,512]{1,0:T(8,128)S(1)}, u32[]{:S(2)}, u32[]{:S(2)}) collective-permute-start(f32[16,512]{1,0:T(8,128)S(1)} %fusion), channel_id=1, source_target_pairs={{0,8},{1,9},{2,10},{3,11},{4,12},{5,13},{6,14},{7,15},{8,16},{9,17... | collective-permute-start | bytes 98312
  1572.9 27.1 %collective-permute-start.8 = (f32[16,512]{1,0:T(8,128)S(1)}, f32[16,512]{1,0:T(8,128)S(1)}, u32[]{:S(2)}, u32[]{:S(2)}) collective-permute-start(f32[16,512]{1,0:T(8,128)S(1)} %fusion), channel_id=1, source_target_pairs={{0,9},{1,10},{2,11},{3,12},{4,13},{5,14},{6,15},{7,16},{8,17},{9,1... | collective-permute-start | bytes 98312
  1586.0 15.2 collective-permute-start.9
  (28 other events, 1520.8 us)
where the time goes:
time: 1630 us
  blocking collectives  1030 us (63%)
  starting transfers between devices  487 us (30%)
  other arithmetic  59.6 us (4%)
  local copies, waits for them, and re-layouts  26 us (2%)
    unnamed x1, blocking collectives  683 us
    unnamed x64, starting transfers between devices  487 us
    all_gather x1, blocking collectives, on_device(): all_points = lax.all_gather(local_points, ('ga', 'orb'), axis=1, tiled=True)  352 us
    convert_element_type x6, other arithmetic, add_panel(): jnp.cos(angle).astype(jnp.bfloat16)  55.8 us
  transfers between devices with their start and end apart: 64, of which 0 were waited for; matrix products, arithmetic and copies ran while one was open for 0% of the time, Pallas kernels for 0%

commit v1 on v0

v1 whole, which is shorter than its diff:
```python
import functools

import jax
import jax.numpy as jnp
from jax import lax
from jax.experimental import pallas as pl
from jax.experimental.pallas import tpu as pltpu
from jax.sharding import PartitionSpec as P

AXES = ("ga", "orb")
S1, S3, S5 = 6.28128008, -41.09524258, 73.58551341
A0, A1 = S1 / S5, S3 / S5
T = (0.15902982, -0.05111658, 0.02327871, -0.00620489)


def pack_kernel(rot, asg, inv, elec, ion, table, msg, scale):
    row = inv[...]
    big = jnp.max(jnp.abs(row), axis=1, keepdims=True)
    safe = jnp.maximum(big, 1e-30)
    q = jnp.round(row * (32767.0 / safe)).astype(jnp.int32)
    half = row.shape[1] // 2
    words = q[:, :half] * 65536 + q[:, half:]
    scale[...] = jnp.broadcast_to(safe * (1.0 / 32767.0), scale.shape)

    lane = lax.broadcasted_iota(jnp.int32, ion.shape, 1)
    home = jnp.sum(jnp.where(lane == asg[0], ion[...], 0.0), axis=1, keepdims=True)
    off = elec[...] - home
    radius = jnp.sqrt(jnp.sum(off * off, axis=0, keepdims=True))
    x = home + radius * table[0]
    x = x - jnp.round(x)
    y = x * 16384.0
    hi = jnp.round(y)
    lo = jnp.round((y - hi) * 32768.0)
    pw = hi.astype(jnp.int32) * 65536 + lo.astype(jnp.int32)
    flat = jnp.concatenate([pw[0:1], pw[1:2], pw[2:3]], axis=1)
    used = 3 * flat.shape[1]
    coords = jnp.concatenate(
        [flat, flat, flat, jnp.zeros((1, 128 - used), jnp.int32)], axis=1
    )
    r = lax.broadcasted_iota(jnp.int32, (24, 128), 0) % 3
    tile = jnp.where(
        r == 0,
        jnp.broadcast_to(words[:, :128], (24, 128)),
        jnp.where(
            r == 1,
            jnp.broadcast_to(words[:, 128:], (24, 128)),
            jnp.broadcast_to(coords, (24, 128)),
        ),
    )
    for i in range(msg.shape[0] // 24):
        msg[pl.ds(24 * i, 24), :] = tile


def pack(rotation, assignment, inverse_rows, elec_pos, ion_pos, quad_table, n):
    q = quad_table.shape[2]
    grid_spec = pltpu.PrefetchScalarGridSpec(
        num_scalar_prefetch=2,
        grid=(1,),
        in_specs=[
            pl.BlockSpec(inverse_rows.shape, lambda i, r, a: (0, 0)),
            pl.BlockSpec(elec_pos.shape, lambda i, r, a: (0, 0)),
            pl.BlockSpec(ion_pos.shape, lambda i, r, a: (0, 0)),
            pl.BlockSpec((1, 3, q), lambda i, r, a: (r[0], 0, 0)),
        ],
        out_specs=[
            pl.BlockSpec((3 * n, 128), lambda i, r, a: (0, 0)),
            pl.BlockSpec((1, 128), lambda i, r, a: (0, 0)),
        ],
    )
    return pl.pallas_call(
        pack_kernel,
        grid_spec=grid_spec,
        out_shape=[
            jax.ShapeDtypeStruct((3 * n, 128), jnp.int32),
            jax.ShapeDtypeStruct((1, 128), jnp.float32),
        ],
        name="pack",
    )(rotation, assignment, inverse_rows, elec_pos, ion_pos, quad_table)


def split16(word):
    low = (word << 16) >> 16
    high = (word - low) >> 16
    return high, low


def two_bf16(v):
    top = (v + 128) >> 8
    rest = v - (top << 8)
    return (top << 8).astype(jnp.float32).astype(jnp.bfloat16), rest.astype(
        jnp.float32
    ).astype(jnp.bfloat16)


NT = (((1,), (1,)), ((), ()))


def wave_kernel(msg, coef, triples, out, ih, il, pts, bt, amp, phi, u):
    n = msg.shape[0] // 3
    waves = triples.shape[1]
    q = out.shape[1]
    for i in range(2):
        high, low = split16(msg[pl.ds(i, n, stride=3), :])
        for j, v in ((i, high), (i + 2, low)):
            a, b = two_bf16(v)
            ih[:, 128 * j : 128 * j + 128] = a
            il[:, 128 * j : 128 * j + 128] = b
    high, low = split16(msg[pl.ds(2, n, stride=3), :])
    p1 = (high + 64) >> 7
    p2 = high - (p1 << 7)
    p3 = (low + 64) >> 7
    lane = lax.broadcasted_iota(jnp.int32, (n, 128), 1)
    w3 = 3 * q
    parts = jnp.where(lane < w3, p1, jnp.where(lane < 2 * w3, p2, p3))
    parts = jnp.where(lane < 3 * w3, parts, 0).astype(jnp.float32)
    which = (lane % w3) % q
    for k in range(q):
        pts[k * n : (k + 1) * n, :] = jnp.where(which == k, parts, 0.0).astype(jnp.bfloat16)
    tr = triples[...].astype(jnp.float32)
    r = lax.broadcasted_iota(jnp.int32, (128, waves), 0)
    axis = (r % w3) // q
    unit = jnp.where(r < w3, 2.0**-7, jnp.where(r < 2 * w3, 2.0**-14, 2.0**-22))
    b = jnp.where(axis == 0, tr[0:1], jnp.where(axis == 1, tr[1:2], tr[2:3])) * unit
    bt[...] = b.T.astype(jnp.bfloat16)

    step = 128

    def weigh(i, c):
        rows = pl.ds(pl.multiple_of(i * step, step), step)
        w = []
        for s in range(2):
            cs = coef[s, rows, :]
            w.append(
                lax.dot_general(cs, ih[...], NT, preferred_element_type=jnp.float32)
                + lax.dot_general(cs, il[...], NT, preferred_element_type=jnp.float32)
            )
        a, b = w
        aa, ab = jnp.abs(a), jnp.abs(b)
        big = jnp.maximum(jnp.maximum(aa, ab), 1e-30)
        t = jnp.minimum(aa, ab) / big
        t2 = t * t
        ang = ((T[3] * t2 + T[2]) * t2 + T[1]) * t2 + T[0]
        ang = ang * t
        ang = jnp.where(ab > aa, 0.25 - ang, ang)
        ang = jnp.where(a < 0.0, 0.5 - ang, ang)
        ang = jnp.where(b < 0.0, -ang, ang)
        phi[rows, :] = ang
        amp[rows, :] = big * jnp.sqrt(1.0 + t2) * (-S5)
        return c

    lax.fori_loop(0, waves // step, weigh, 0)

    for k in range(q):
        u[k] = lax.dot_general(
            bt[...], pts[k * n : (k + 1) * n, :], NT, preferred_element_type=jnp.float32
        )

    for h in range(n // 128):
        cols = slice(128 * h, 128 * h + 128)

        def tile(i, acc):
            rows = pl.ds(pl.multiple_of(i * 8, 8), 8)
            ph = phi[rows, cols]
            am = amp[rows, cols]
            new = []
            for k in range(q):
                v = u[k, rows, cols] - ph
                v = jnp.abs(v - jnp.round(v)) - 0.25
                s = v * v
                new.append(acc[k] + (((s + A1) * s + A0) * v) * am)
            return tuple(new)

        zero = jnp.zeros((8, 128), jnp.float32)
        acc = lax.fori_loop(0, waves // 8, tile, (zero,) * q, unroll=2)
        sums = [jnp.sum(a, axis=0, keepdims=True) for a in acc]
        sums.append(jnp.zeros((128 - q, 128), jnp.float32))
        out[cols, :] = jnp.concatenate(sums, axis=0).T[:, :q]


def partial_ratios(msg, coefficients, triples, n, q):
    waves = triples.shape[1]
    orbitals = coefficients.shape[2]
    vmem = pl.BlockSpec(memory_space=pltpu.VMEM)
    return pl.pallas_call(
        wave_kernel,
        out_shape=jax.ShapeDtypeStruct((n, q), jnp.float32),
        in_specs=[vmem] * 3,
        out_specs=vmem,
        scratch_shapes=[
            pltpu.VMEM((n, orbitals), jnp.bfloat16),
            pltpu.VMEM((n, orbitals), jnp.bfloat16),
            pltpu.VMEM((q * n, 128), jnp.bfloat16),
            pltpu.VMEM((waves, 128), jnp.bfloat16),
            pltpu.VMEM((waves, n), jnp.float32),
            pltpu.VMEM((waves, n), jnp.float32),
            pltpu.VMEM((q, waves, n), jnp.float32),
        ],
        compiler_params=pltpu.CompilerParams(vmem_limit_bytes=40 << 20),
        name="waves",
    )(msg, coefficients, triples)


def on_device(
    coefficients, triples, elec_pos, ion_pos, assignment, rotation, quad_table, inverse_rows, n
):
    q = quad_table.shape[2]
    msg, scale = pack(rotation, assignment, inverse_rows, elec_pos, ion_pos, quad_table, n)
    got = lax.all_to_all(msg.reshape(n, 1, 384), AXES, 0, 0, tiled=True)
    part = partial_ratios(got.reshape(3 * n, 128), coefficients, triples, n, q)
    back = lax.all_to_all(part.reshape(n, 1, q), AXES, 0, 0, tiled=True)
    return jnp.sum(back, axis=0) * scale[:, :1]


def solution(mesh):
    n = mesh.shape["ga"] * mesh.shape["orb"]
    return jax.shard_map(
        functools.partial(on_device, n=n),
        mesh=mesh,
        in_specs=(
            P(None, AXES, None),
            P(None, AXES),
            P(None, AXES),
            P(),
            P(AXES),
            P(AXES),
            P(),
            P(AXES, None),
        ),
        out_specs=P(AXES, None),
        check_vma=False,
    )
```

time: 1630 us -> 76.7 us (0.05)
  blocking collectives: 1030 us -> 52.4 us
  starting transfers between devices: 487 us -> 0 us
  other arithmetic: 59.6 us -> 0.83 us
  local copies, waits for them, and re-layouts: 26 us -> 5.19 us
  Pallas kernels: 0 us -> 16.6 us
    unnamed x1 -> x0, blocking collectives: 683 us -> none
    unnamed x64 -> x0, starting transfers between devices: 487 us -> none
    all_gather x1 -> x0, blocking collectives: 352 us -> none  [on_device(): all_points = lax.all_gather(local_points, ('ga', 'orb'), axis=1, tiled=True)]
    convert_element_type x6 -> x0, other arithmetic: 55.8 us -> none  [add_panel(): jnp.cos(angle).astype(jnp.bfloat16)]
    all_to_all x0 -> x2, blocking collectives: none -> 52.4 us  [the longest x1 33.8 us: on_device(): got = lax.all_to_all(msg.reshape(n, 1, 384), AXES, 0, 0, tiled=True)]
    unnamed x48 -> x8, local copies, waits for them, and re-layouts: 25.6 us -> 5.19 us
    pallas_call x0 -> x2, Pallas kernels: none -> 16.6 us  [the longest x1 14.8 us: partial_ratios(): pl.pallas_call(wave_kernel, out_shape=jax.ShapeDtypeStruct((n, q), jnp.fl...]
  transfers between devices with their start and end apart: 64 -> 0, of which waited for: 0 -> 0; matrix products, arithmetic and copies ran while one was open for 0% -> 0% of each run, Pallas kernels for 0% -> 0%
where the time goes in v1:
time: 76.7 us; the launch traced here: 76.4 us
  blocking collectives  52.4 us (68%)
  Pallas kernels  16.6 us (22%)
  local copies, waits for them, and re-layouts  5.19 us (7%)
  between operations  1.3 us (2%)
  other arithmetic  0.83 us (1%)
    all_to_all x1, blocking collectives, on_device(): got = lax.all_to_all(msg.reshape(n, 1, 384), AXES, 0, 0, tiled=True)  33.8 us
    all_to_all x1, blocking collectives, on_device(): back = lax.all_to_all(part.reshape(n, 1, q), AXES, 0, 0, tiled=True)  18.6 us
    pallas_call x1, Pallas kernels, partial_ratios(): pl.pallas_call(wave_kernel, out_shape=jax.ShapeDtypeStruct((n, q), jnp.fl...  14.8 us
    unnamed x8, local copies, waits for them, and re-layouts  5.19 us
    pallas_call x1, Pallas kernels, pack(): pl.pallas_call(pack_kernel, grid_spec=grid_spec, out_shape=[jax.ShapeDtyp...  1.82 us

profile of v1, /device:TPU:1, one launch (start us, length us, event | category | flops | bytes accessed | tf_op | source)
XLA Modules:
  0.0 76.4 jit_solution(8799751732781351315)
XLA Ops:
  1.3 1.3 %copy.11.elec = f32[3,1]{1,0:T(4,128)} copy(f32[3,1]{0,1:T(1,128)} %param.10) | data formatting | bytes 24 | tf_op args[2]
  2.6 1.5 %copy.12.table = f32[64,3,12]{2,1,0:T(4,128)} copy(f32[64,3,12]{0,2,1:T(8,128)} %param.14) | data formatting | bytes 18432 | tf_op args[6]
  4.1 1.8 %pack.1 = (s32[768,128]{1,0:T(8,128)}, f32[1,128]{1,0:T(1,128)}) custom-call(s32[1]{0:T(128)S(6)} %copy.16.rot, s32[1]{0:T(128)S(6)} %copy.15.asg, f32[1,512]{1,0:T(1,128)} %inv.1, f32[3,1]{1,0:T(4,128)} %copy.11.elec, f32[3,128]{1,0:T(4,128)} %ion.1, f32[64,3,12]{2,1,0:T(4,128)} %copy.12.table), custom_call_target="tpu_custom_call" | custom-call | tf_op jit(solution)/shard_map/pack/pallas_call | solution.py:70
  5.9 0.0 copy-start.2
  5.9 33.8 %all_to_all.10 = s32[256,1,384]{2,1,0:T(1,128)S(1)} all-to-all(s32[256,1,384]{2,1,0:T(1,128)} %bitcast.11), channel_id=1, replica_groups=mesh['ga'=4,'orb'=64] {'ga','orb'}, dimensions={0} | all-to-all | bytes 786432 | tf_op jit(solution)/shard_map/all_to_all | solution.py:208
  39.7 0.0 copy-start
  39.7 1.7 %copy-done = bf16[2,1152,512]{2,1,0:T(8,128)(2,1)S(1)} copy-done((bf16[2,1152,512]{2,1,0:T(8,128)(2,1)S(1)}, bf16[2,1152,512]{2,1,0:T(8,128)(2,1)}, u32[]{:S(2)}) %copy-start) | copy-done | bytes 2359320
  41.4 0.0 copy-start.1
  41.4 0.7 copy-done.1
  42.1 14.8 %waves.1 = f32[256,12]{1,0:T(8,128)S(1)} custom-call(s32[768,128]{1,0:T(8,128)S(1)} %bitcast.9, bf16[2,1152,512]{2,1,0:T(8,128)(2,1)S(1)} %copy-done, s32[3,1152]{1,0:T(4,128)S(1)} %copy-done.1), custom_call_target="tpu_custom_call" | custom-call | tf_op jit(solution)/shard_map/waves/pallas_call | solution.py:184
  56.9 18.6 %all_to_all.11 = f32[256,1,12]{2,1,0:T(1,128)S(1)} all-to-all(f32[256,1,12]{2,1,0:T(1,128)S(1)} %bitcast.10), channel_id=1, replica_groups=mesh['ga'=4,'orb'=64] {'ga','orb'}, dimensions={0} | all-to-all | bytes 24576 | tf_op jit(solution)/shard_map/all_to_all | solution.py:210
  75.5 0.3 reduce_sum.9
  75.8 0.0 copy-done.2
  75.8 0.5 multiply_bitcast_fusion
Async XLA Ops:
  5.9 69.9 %copy-start.2 = (f32[1,128]{1,0:T(1,128)S(1)}, f32[1,128]{1,0:T(1,128)}, u32[]{:S(2)}) copy-start(f32[1,128]{1,0:T(1,128)} %get-tuple-element.8) | copy-start | bytes 1540
  39.7 1.7 %copy-start = (bf16[2,1152,512]{2,1,0:T(8,128)(2,1)S(1)}, bf16[2,1152,512]{2,1,0:T(8,128)(2,1)}, u32[]{:S(2)}) copy-start(bf16[2,1152,512]{2,1,0:T(8,128)(2,1)} %coef.1) | copy-start | bytes 7077892
  41.4 0.7 copy-start.1

commit v2 on v0

v2 whole, which is shorter than its diff:
```python
import functools

import jax
import jax.numpy as jnp
from jax import lax
from jax.experimental import pallas as pl
from jax.experimental.pallas import tpu as pltpu
from jax.sharding import PartitionSpec as P

AXES = ("ga", "orb")
UP = 2.0**40
CHUNKS = (128, 256, 256, 256, 128, 128)
S1, S3, S5 = 6.28128008, -41.09524258, 73.58551341
A0, A1 = S1 / S5, S3 / S5
T = (0.15911832, 0.02740563, 0.00639816, 0.01881423)


def pack_kernel(rot, asg, inv, elec, ion, table, msg, scale):
    row = inv[...]
    big = jnp.max(jnp.abs(row), axis=1, keepdims=True)
    safe = jnp.maximum(big, 1e-30)
    n16 = jnp.round(row * (32767.0 / safe)).astype(jnp.int32)
    half = row.shape[1] // 2
    words = n16[:, :half] * 65536 + n16[:, half:]
    scale[...] = jnp.broadcast_to(safe * (1.0 / 32767.0 / UP), scale.shape)

    lane = lax.broadcasted_iota(jnp.int32, ion.shape, 1)
    home = jnp.sum(jnp.where(lane == asg[0], ion[...], 0.0), axis=1, keepdims=True)
    turn = lax.broadcasted_iota(jnp.int32, table.shape[1:], 1)
    total = 0.0
    homes = []
    for c in range(3):
        h = home[c : c + 1, :]
        off = elec[:, c : c + 1] - h
        homes.append(h)
        total = total + off * off
    radius = jnp.sqrt(total)
    rows = []
    for c in range(3):
        shift = jnp.sum(jnp.where(turn == rot[0], table[c], 0.0), axis=1, keepdims=True)
        x = homes[c] + radius * shift
        x = x - jnp.round(x)
        y = x * 16384.0
        hi = jnp.round(y)
        lo = jnp.round((y - hi) * 32768.0)
        rows.append(hi.astype(jnp.int32) * 65536 + lo.astype(jnp.int32))
    flat = jnp.concatenate(rows, axis=0)
    used = 3 * flat.shape[0]
    column = jnp.concatenate([flat, flat, flat, jnp.zeros((128 - used, 1), jnp.int32)], axis=0)
    square = jnp.broadcast_to(column, (128, 128)).T
    coords = square[:24]
    r = lax.broadcasted_iota(jnp.int32, (24, 128), 0) % 3
    tile = jnp.where(
        r == 0,
        jnp.broadcast_to(words[:, :128], (24, 128)),
        jnp.where(r == 1, jnp.broadcast_to(words[:, 128:], (24, 128)), coords),
    )
    for i in range(msg.shape[0] // 24):
        msg[pl.ds(24 * i, 24), :] = tile


def pack(rotation, assignment, inverse_rows, elec_pos, ion_pos, quad_table, n):
    vmem = pl.BlockSpec(memory_space=pltpu.VMEM)
    smem = pl.BlockSpec(memory_space=pltpu.SMEM)
    return pl.pallas_call(
        pack_kernel,
        in_specs=[smem, smem, vmem, vmem, vmem, vmem],
        out_specs=[vmem, vmem],
        out_shape=[
            jax.ShapeDtypeStruct((3 * n, 128), jnp.int32),
            jax.ShapeDtypeStruct((1, 128), jnp.float32),
        ],
        name="pack",
    )(
        rotation,
        assignment,
        inverse_rows,
        elec_pos.T,
        ion_pos,
        jnp.transpose(quad_table, (1, 2, 0)),
    )


def split16(word):
    low = (word << 16) >> 16
    high = (word - low) >> 16
    return high, low


def two_bf16(v):
    f = v.astype(jnp.float32) * UP
    top = f.astype(jnp.bfloat16)
    return top, (f - top.astype(jnp.float32)).astype(jnp.bfloat16)


NT = (((1,), (1,)), ((), ()))
TN = (((0,), (0,)), ((), ()))


def wave_kernel(
    own, mate, coef_hbm, triples_hbm, out, coef, triples, ih, il, parts, bt, amp, phi, ua, ub, rows_out, sem
):
    n = ih.shape[0]
    half = n // 2
    waves = triples.shape[1]
    q = out.shape[1]
    first = CHUNKS[0]
    copies = [pltpu.make_async_copy(triples_hbm, triples, sem.at[0])]
    for s in range(2):
        for lo, size in ((0, first), (first, waves - first)):
            copies.append(
                pltpu.make_async_copy(
                    coef_hbm.at[s, pl.ds(lo, size), :],
                    coef.at[s, pl.ds(lo, size), :],
                    sem.at[len(copies)],
                )
            )
    for c in (0, 1, 3, 2, 4):
        copies[c].start()
    odd = lax.axis_index("orb") % 2
    w3 = 3 * q

    def words(h, r0, i):
        at = pl.ds(i + 3 * r0, 32, stride=3)
        return jnp.where(odd == h, own[at, :], mate[at, :])

    for h in range(2):
        for r0 in range(0, half, 32):
            dst = slice(h * half + r0, h * half + r0 + 32)
            for i in range(2):
                high, low = split16(words(h, r0, i))
                for j, v in ((i, high), (i + 2, low)):
                    ih[dst, 128 * j : 128 * j + 128], il[dst, 128 * j : 128 * j + 128] = two_bf16(v)

    def weigh(lo, size):
        rows = slice(lo, lo + size)
        for s, ref in ((0, amp), (1, phi)):
            cs = coef[s, rows, :]
            ref[rows, :] = lax.dot_general(
                cs, ih[...], NT, preferred_element_type=jnp.float32
            ) + lax.dot_general(cs, il[...], NT, preferred_element_type=jnp.float32)

    copies[1].wait()
    copies[3].wait()
    weigh(0, first)

    lane = lax.broadcasted_iota(jnp.int32, (32, 128), 1)
    for h in range(2):
        for r0 in range(0, half, 32):
            high, low = split16(words(h, r0, 2))
            p1 = (high + 64) >> 7
            p2 = high - (p1 << 7)
            p3 = (low + 64) >> 7
            v = jnp.where(lane < w3, p1, jnp.where(lane < 2 * w3, p2, p3))
            parts[h * half + r0 : h * half + r0 + 32, :] = v.astype(jnp.float32).astype(jnp.bfloat16)
    which = (lane[:1] % w3) % q
    copies[0].wait()
    r = lax.broadcasted_iota(jnp.int32, (8, 128), 1)
    axis = (r % w3) // q
    unit = jnp.where(r < w3, 2.0**-7, jnp.where(r < 2 * w3, 2.0**-14, 2.0**-22))
    pick = (lax.broadcasted_iota(jnp.int32, (8, 128), 0) == axis) & (r < 3 * w3)
    spread = jnp.where(pick, unit, 0.0).astype(jnp.bfloat16)
    tr = triples[...].astype(jnp.float32)
    tr = jnp.concatenate([tr, jnp.zeros((5, waves), jnp.float32)], axis=0).T.astype(jnp.bfloat16)
    bt[...] = jnp.dot(tr, spread, preferred_element_type=jnp.float32).astype(jnp.bfloat16)

    def polar(lo, size):
        for g in range(lo, lo + size, 16):
            rows = slice(g, g + 16)
            a, b = amp[rows, :], phi[rows, :]
            aa, ab = jnp.abs(a), jnp.abs(b)
            h = jnp.maximum(a * a + b * b, 1e-36)
            r = lax.rsqrt(h)
            amp[rows, :] = h * r * (-S5)
            t = jnp.minimum(aa, ab) * r
            t2 = t * t
            ang = ((T[3] * t2 + T[2]) * t2 + T[1]) * t2 + T[0]
            ang = ang * t
            ang = jnp.where(ab > aa, 0.25 - ang, ang)
            ang = jnp.where(a < 0.0, 0.5 - ang, ang)
            phi[rows, :] = jnp.where(b < 0.0, -ang, ang)

    def angles(k, ref):
        mask = jnp.where(which == k, 1.0, 0.0).astype(jnp.bfloat16)
        ref[...] = lax.dot_general(
            bt[...], parts[...] * mask, NT, preferred_element_type=jnp.float32
        )

    def contract(k, ref):
        acc = jnp.zeros((8, n), jnp.float32)
        for g in range(0, waves, 8):
            rows = slice(g, g + 8)
            v = ref[rows, :] - phi[rows, :]
            v = jnp.abs(v - jnp.round(v)) - 0.25
            s = v * v
            acc = acc + (((s + A1) * s + A0) * v) * amp[rows, :]
        rows_out[pl.ds(k, 1), :] = jnp.sum(acc, axis=0, keepdims=True)

    copies[2].wait()
    copies[4].wait()
    lo = 0
    for size, ahead in zip(CHUNKS, CHUNKS[1:]):
        weigh(lo + size, ahead)
        polar(lo, size)
        lo += size
    angles(0, ua)
    polar(lo, CHUNKS[-1])

    def pair(j, c):
        angles(2 * j + 1, ub)
        contract(2 * j, ua)
        angles(jnp.minimum(2 * j + 2, q - 1), ua)
        contract(2 * j + 1, ub)
        return c

    lax.fori_loop(0, q // 2, pair, 0)
    for h in range(2):
        turned = rows_out[:, h * half : h * half + half].T
        out[pl.ds(h, half, stride=2), :] = turned[:, :q]


def partial_ratios(own, mate, coefficients, triples, n, q):
    waves = triples.shape[1]
    orbitals = coefficients.shape[2]
    vmem = pl.BlockSpec(memory_space=pltpu.VMEM)
    hbm = pl.BlockSpec(memory_space=pltpu.HBM)
    return pl.pallas_call(
        wave_kernel,
        out_shape=jax.ShapeDtypeStruct((n, q), jnp.float32),
        in_specs=[vmem, vmem, hbm, hbm],
        out_specs=vmem,
        scratch_shapes=[
            pltpu.VMEM(coefficients.shape, jnp.bfloat16),
            pltpu.VMEM(triples.shape, jnp.int32),
            pltpu.VMEM((n, orbitals), jnp.bfloat16),
            pltpu.VMEM((n, orbitals), jnp.bfloat16),
            pltpu.VMEM((n, 128), jnp.bfloat16),
            pltpu.VMEM((waves, 128), jnp.bfloat16),
            pltpu.VMEM((waves, n), jnp.float32),
            pltpu.VMEM((waves, n), jnp.float32),
            pltpu.VMEM((waves, n), jnp.float32),
            pltpu.VMEM((waves, n), jnp.float32),
            pltpu.VMEM((128, n), jnp.float32),
            pltpu.SemaphoreType.DMA((5,)),
        ],
        compiler_params=pltpu.CompilerParams(vmem_limit_bytes=52 << 20),
        name="waves",
    )(own, mate, coefficients, triples)


def on_device(
    coefficients, triples, elec_pos, ion_pos, assignment, rotation, quad_table, inverse_rows, n
):
    q = quad_table.shape[2]
    half = n // 2
    msg, scale = pack(rotation, assignment, inverse_rows, elec_pos, ion_pos, quad_table, half)
    sides = [list(range(c, n, 2)) for c in range(2)]
    own = lax.all_to_all(
        msg.reshape(half, 1, 384), AXES, 0, 0, axis_index_groups=sides, tiled=True
    ).reshape(3 * half, 128)
    mate = lax.ppermute(own, AXES, [(i, i ^ 1) for i in range(n)])
    part = partial_ratios(own, mate, coefficients, triples, n, q)
    back = lax.all_to_all(part.reshape(n, 1, q), AXES, 0, 0, tiled=True)
    return jnp.sum(back * scale[0, 0], axis=0)


def solution(mesh):
    n = mesh.shape["ga"] * mesh.shape["orb"]
    return jax.shard_map(
        functools.partial(on_device, n=n),
        mesh=mesh,
        in_specs=(
            P(None, AXES, None),
            P(None, AXES),
            P(None, AXES),
            P(),
            P(AXES),
            P(AXES),
            P(),
            P(AXES, None),
        ),
        out_specs=P(AXES, None),
        check_vma=False,
    )
```

time: 1630 us -> 65.2 us (0.04)
  blocking collectives: 1030 us -> 45.6 us
  starting transfers between devices: 487 us -> 2.85 us
  other arithmetic: 59.6 us -> 0.83 us
  local copies, waits for them, and re-layouts: 26 us -> 0.73 us
    unnamed x1 -> x0, blocking collectives: 683 us -> none
    unnamed x64 -> x0, starting transfers between devices: 487 us -> none
    all_gather x1 -> x0, blocking collectives: 352 us -> none  [on_device(): all_points = lax.all_gather(local_points, ('ga', 'orb'), axis=1, tiled=True)]
    convert_element_type x6 -> x0, other arithmetic: 55.8 us -> none  [add_panel(): jnp.cos(angle).astype(jnp.bfloat16)]
    all_to_all x0 -> x2, blocking collectives: none -> 45.6 us  [the longest x1 27.5 us: on_device(): lax.all_to_all(msg.reshape(half, 1, 384), AXES, 0, 0, axis_index_groups=s...]
    unnamed x48 -> x4, local copies, waits for them, and re-layouts: 25.6 us -> 0.73 us
  transfers between devices with their start and end apart: 64 -> 1, of which waited for: 0 -> 1; matrix products, arithmetic and copies ran while one was open for 0% -> 0% of each run, Pallas kernels for 0% -> 0%
where the time goes in v2:
time: 65.2 us; the launch traced here: 64.9 us
  blocking collectives  45.6 us (70%)
  Pallas kernels  12.5 us (19%)
  starting transfers between devices  2.85 us (4%)
  between operations  1.31 us (2%)
  waiting for transfers between devices  1.07 us (2%)
  other arithmetic  0.83 us (1%)
  local copies, waits for them, and re-layouts  0.73 us (1%)
    all_to_all x1, blocking collectives, on_device(): lax.all_to_all(msg.reshape(half, 1, 384), AXES, 0, 0, axis_index_groups=s...  27.5 us
    all_to_all x1, blocking collectives, on_device(): back = lax.all_to_all(part.reshape(n, 1, q), AXES, 0, 0, tiled=True)  18.1 us
    pallas_call x1, Pallas kernels, partial_ratios(): pl.pallas_call(wave_kernel, out_shape=jax.ShapeDtypeStruct((n, q), jnp.fl...  10.7 us
    ppermute x1, starting transfers between devices, on_device(): mate = lax.ppermute(own, AXES, [(i, i ^ 1) for i in range(n)])  2.85 us
    pallas_call x1, Pallas kernels, pack(): pl.pallas_call(pack_kernel, in_specs=[smem, smem, vmem, vmem, vmem, vmem]...  1.8 us
  transfers between devices with their start and end apart: 1, of which 1 were waited for; matrix products, arithmetic and copies ran while one was open for 0% of the time, Pallas kernels for 0%

profile of v2, /device:TPU:1, one launch (start us, length us, event | category | flops | bytes accessed | tf_op | source)
XLA Modules:
  0.0 64.9 jit_solution(681841310325360495)
XLA Ops:
  1.3 1.8 %pack.1 = (s32[384,128]{1,0:T(8,128)}, f32[1,128]{1,0:T(1,128)}) custom-call(s32[1]{0:T(128)S(6)} %copy.12.rot, s32[1]{0:T(128)S(6)} %copy.11.asg, f32[1,512]{1,0:T(1,128)} %inv.1, f32[1,3]{1,0:T(1,128)} %bitcast.15, f32[3,128]{1,0:T(4,128)} %ion.1, f32[3,12,64]{2,1,0:T(8,128)} %bitcast.14), custom_call_target="tpu_custom_call" | custom-call | tf_op jit(solution)/shard_map/pack/pallas_call | solution.py:65
  3.1 0.0 copy-start.1
  3.1 27.5 %all_to_all.10 = s32[128,1,384]{2,1,0:T(1,128)S(1)} all-to-all(s32[128,1,384]{2,1,0:T(1,128)} %bitcast.13), channel_id=1, replica_groups={{0,2,4,6,8,10,12,14,16,18,20,22,24,26,28,30,32,34,36,38,40,42,44,46,48,..., dimensions={0} | all-to-all | bytes 393216 | tf_op jit(solution)/shard_map/all_to_all | solution.py:258
  30.6 2.8 %collective-permute-start = (s32[384,128]{1,0:T(8,128)S(1)}, s32[384,128]{1,0:T(8,128)S(1)}, u32[]{:S(2)}, u32[]{:S(2)}) collective-permute-start(s32[384,128]{1,0:T(8,128)S(1)} %bitcast.10), channel_id=1, source_target_pairs={{0,1},{1,0},{2,3},{3,2},{4,5},{5,4},{6,7},{7,6},{8,9},{9,8},{10,11... | collective-permute-start | bytes 589832 | tf_op jit(solution)/shard_map/ppermute | solution.py:261
  33.5 1.1 %collective-permute-done.mate = s32[384,128]{1,0:T(8,128)S(1)} collective-permute-done((s32[384,128]{1,0:T(8,128)S(1)}, s32[384,128]{1,0:T(8,128)S(1)}, u32[]{:S(2)}, u32[]{:S(2)}) %collective-permute-start) | collective-permute-done | bytes 196640 | tf_op jit(solution)/shard_map/ppermute | solution.py:261
  34.5 0.0 copy-start
  34.5 0.7 %copy-done = s32[3,1152]{1,0:T(4,128)S(1)} copy-done((s32[3,1152]{1,0:T(4,128)S(1)}, s32[3,1152]{1,0:T(4,128)}, u32[]{:S(2)}) %copy-start) | copy-done | bytes 13848
  35.3 10.7 %waves.1 = f32[256,12]{1,0:T(8,128)S(1)} custom-call(s32[384,128]{1,0:T(8,128)S(1)} %bitcast.11, s32[384,128]{1,0:T(8,128)S(1)} %collective-permute-done.mate, bf16[2,1152,512]{2,1,0:T(8,128)(2,1)} %coef_hbm.1, s32[3,1152]{1,0:T(4,128)S(1)} %copy-done), custom_call_target="tpu_custom_call" | custom-call | tf_op jit(solution)/shard_map/waves/pallas_call | solution.py:227
  45.9 18.1 %all_to_all.11 = f32[256,1,12]{2,1,0:T(1,128)S(1)} all-to-all(f32[256,1,12]{2,1,0:T(1,128)S(1)} %bitcast.12), channel_id=1, replica_groups=mesh['ga'=4,'orb'=64] {'ga','orb'}, dimensions={0} | all-to-all | bytes 24576 | tf_op jit(solution)/shard_map/all_to_all | solution.py:263
  64.0 0.0 copy-done.1
  64.0 0.8 %multiply_reduce_fusion = f32[12]{0:T(128)} fusion(f32[256,1,12]{2,1,0:T(1,128)S(1)} %all_to_all.11, f32[]{:T(128)S(1)} %bitcast.16), kind=kLoop, calls=%fused_computation | loop fusion | flops 6132 | bytes 12340 | tf_op jit(solution)/shard_map/reduce_sum | solution.py:264
Async XLA Ops:
  3.1 60.9 %copy-start.1 = (f32[1,128]{1,0:T(1,128)S(1)}, f32[1,128]{1,0:T(1,128)}, u32[]{:S(2)}) copy-start(f32[1,128]{1,0:T(1,128)} %get-tuple-element.8) | copy-start | bytes 1540
  30.6 3.9 %collective-permute-start = (s32[384,128]{1,0:T(8,128)S(1)}, s32[384,128]{1,0:T(8,128)S(1)}, u32[]{:S(2)}, u32[]{:S(2)}) collective-permute-start(s32[384,128]{1,0:T(8,128)S(1)} %bitcast.10), channel_id=1, source_target_pairs={{0,1},{1,0},{2,3},{3,2},{4,5},{5,4},{6,7},{7,6},{8,9},{9,8},{10,11... | collective-permute-start | bytes 589832 | tf_op jit(solution)/shard_map/ppermute | solution.py:261
  34.5 0.7 %copy-start = (s32[3,1152]{1,0:T(4,128)S(1)}, s32[3,1152]{1,0:T(4,128)}, u32[]{:S(2)}) copy-start(s32[3,1152]{1,0:T(4,128)} %triples_hbm.1) | copy-start | bytes 41476

commit v3 on v2

--- a/solution.py
+++ b/solution.py
@@ -9,20 +9,25 @@
 
 AXES = ("ga", "orb")
 UP = 2.0**40
+KEPT_ROWS = 640
 CHUNKS = (128, 256, 256, 256, 128, 128)
-S1, S3, S5 = 6.28128008, -41.09524258, 73.58551341
-A0, A1 = S1 / S5, S3 / S5
+C0, C1, C2 = 0.26392367, -1.2978812, 28.72800057
+MEAN = 0.0348596450351644
 T = (0.15911832, 0.02740563, 0.00639816, 0.01881423)
 
 
-def pack_kernel(rot, asg, inv, elec, ion, table, msg, scale):
+def pack_kernel(rot, asg, inv, elec, ion, table, triples, msg, kept, eight, sem):
+    eight[...] = jnp.zeros_like(eight)
+    eight[0:3, :] = triples[...]
+    keep = pltpu.make_async_copy(eight, kept.at[pl.ds(0, 8), :], sem)
+    keep.start()
     row = inv[...]
     big = jnp.max(jnp.abs(row), axis=1, keepdims=True)
     safe = jnp.maximum(big, 1e-30)
-    n16 = jnp.round(row * (32767.0 / safe)).astype(jnp.int32)
+    power = jnp.floor(jnp.log2(32767.0 / safe))
+    n16 = jnp.clip(jnp.round(row * jnp.exp2(power)), -32767.0, 32767.0).astype(jnp.int32)
     half = row.shape[1] // 2
     words = n16[:, :half] * 65536 + n16[:, half:]
-    scale[...] = jnp.broadcast_to(safe * (1.0 / 32767.0 / UP), scale.shape)
 
     lane = lax.broadcasted_iota(jnp.int32, ion.shape, 1)
     home = jnp.sum(jnp.where(lane == asg[0], ion[...], 0.0), axis=1, keepdims=True)
@@ -46,7 +51,9 @@
         rows.append(hi.astype(jnp.int32) * 65536 + lo.astype(jnp.int32))
     flat = jnp.concatenate(rows, axis=0)
     used = 3 * flat.shape[0]
-    column = jnp.concatenate([flat, flat, flat, jnp.zeros((128 - used, 1), jnp.int32)], axis=0)
+    column = jnp.concatenate(
+        [flat, flat, flat, jnp.zeros((127 - used, 1), jnp.int32), power.astype(jnp.int32)], axis=0
+    )
     square = jnp.broadcast_to(column, (128, 128)).T
     coords = square[:24]
     r = lax.broadcasted_iota(jnp.int32, (24, 128), 0) % 3
@@ -57,18 +64,23 @@
     )
     for i in range(msg.shape[0] // 24):
         msg[pl.ds(24 * i, 24), :] = tile
-
-
-def pack(rotation, assignment, inverse_rows, elec_pos, ion_pos, quad_table, n):
+    keep.wait()
+
+
+def pack(rotation, assignment, inverse_rows, elec_pos, ion_pos, quad_table, triples, n):
     vmem = pl.BlockSpec(memory_space=pltpu.VMEM)
     smem = pl.BlockSpec(memory_space=pltpu.SMEM)
     return pl.pallas_call(
         pack_kernel,
-        in_specs=[smem, smem, vmem, vmem, vmem, vmem],
-        out_specs=[vmem, vmem],
+        in_specs=[smem, smem, vmem, vmem, vmem, vmem, vmem],
+        out_specs=[vmem, pl.BlockSpec(memory_space=pltpu.HBM)],
         out_shape=[
             jax.ShapeDtypeStruct((3 * n, 128), jnp.int32),
-            jax.ShapeDtypeStruct((1, 128), jnp.float32),
+            jax.ShapeDtypeStruct((KEPT_ROWS, triples.shape[1]), jnp.int32),
+        ],
+        scratch_shapes=[
+            pltpu.VMEM((8, triples.shape[1]), jnp.int32),
+            pltpu.SemaphoreType.DMA,
         ],
         name="pack",
     )(
@@ -78,6 +90,7 @@
         elec_pos.T,
         ion_pos,
         jnp.transpose(quad_table, (1, 2, 0)),
+        triples,
     )
 
 
@@ -98,14 +111,14 @@
 
 
 def wave_kernel(
-    own, mate, coef_hbm, triples_hbm, out, coef, triples, ih, il, parts, bt, amp, phi, ua, ub, rows_out, sem
+    own, mate, coef_hbm, triples_hbm, out, coef, triples, ih, il, parts, bt, amp, phi, ua, ub, rows_out, base, unit_of, sem
 ):
     n = ih.shape[0]
     half = n // 2
     waves = triples.shape[1]
     q = out.shape[1]
     first = CHUNKS[0]
-    copies = [pltpu.make_async_copy(triples_hbm, triples, sem.at[0])]
+    copies = [pltpu.make_async_copy(triples_hbm.at[pl.ds(0, 8), :], triples, sem.at[0])]
     for s in range(2):
         for lo, size in ((0, first), (first, waves - first)):
             copies.append(
@@ -147,7 +160,10 @@
     lane = lax.broadcasted_iota(jnp.int32, (32, 128), 1)
     for h in range(2):
         for r0 in range(0, half, 32):
-            high, low = split16(words(h, r0, 2))
+            word = words(h, r0, 2)
+            scale = jnp.exp2(-word[:, 127:].astype(jnp.float32)) * (1.0 / UP)
+            unit_of[h * half + r0 : h * half + r0 + 32, :] = jnp.broadcast_to(scale, (32, 128))
+            high, low = split16(word)
             p1 = (high + 64) >> 7
             p2 = high - (p1 << 7)
             p3 = (low + 64) >> 7
@@ -160,18 +176,20 @@
     unit = jnp.where(r < w3, 2.0**-7, jnp.where(r < 2 * w3, 2.0**-14, 2.0**-22))
     pick = (lax.broadcasted_iota(jnp.int32, (8, 128), 0) == axis) & (r < 3 * w3)
     spread = jnp.where(pick, unit, 0.0).astype(jnp.bfloat16)
-    tr = triples[...].astype(jnp.float32)
-    tr = jnp.concatenate([tr, jnp.zeros((5, waves), jnp.float32)], axis=0).T.astype(jnp.bfloat16)
+    tr = triples[...].astype(jnp.float32).T.astype(jnp.bfloat16)
     bt[...] = jnp.dot(tr, spread, preferred_element_type=jnp.float32).astype(jnp.bfloat16)
 
-    def polar(lo, size):
-        for g in range(lo, lo + size, 16):
+    def polar(lo, count):
+        total = base[...]
+        for g in range(lo, lo + count, 16):
             rows = slice(g, g + 16)
             a, b = amp[rows, :], phi[rows, :]
             aa, ab = jnp.abs(a), jnp.abs(b)
             h = jnp.maximum(a * a + b * b, 1e-36)
             r = lax.rsqrt(h)
-            amp[rows, :] = h * r * (-S5)
+            size = h * r * C2
+            amp[rows, :] = size
+            total = total + size[:8] + size[8:]
             t = jnp.minimum(aa, ab) * r
             t2 = t * t
             ang = ((T[3] * t2 + T[2]) * t2 + T[1]) * t2 + T[0]
@@ -179,6 +197,7 @@
             ang = jnp.where(ab > aa, 0.25 - ang, ang)
             ang = jnp.where(a < 0.0, 0.5 - ang, ang)
             phi[rows, :] = jnp.where(b < 0.0, -ang, ang)
+        base[...] = total
 
     def angles(k, ref):
         mask = jnp.where(which == k, 1.0, 0.0).astype(jnp.bfloat16)
@@ -191,13 +210,15 @@
         for g in range(0, waves, 8):
             rows = slice(g, g + 8)
             v = ref[rows, :] - phi[rows, :]
-            v = jnp.abs(v - jnp.round(v)) - 0.25
+            v = v - jnp.round(v)
             s = v * v
-            acc = acc + (((s + A1) * s + A0) * v) * amp[rows, :]
-        rows_out[pl.ds(k, 1), :] = jnp.sum(acc, axis=0, keepdims=True)
+            w = (s + C1) * s + C0
+            acc = acc + (w * w) * amp[rows, :]
+        rows_out[pl.ds(k, 1), :] = jnp.sum(acc - base[...], axis=0, keepdims=True)
 
     copies[2].wait()
     copies[4].wait()
+    base[...] = jnp.zeros_like(base)
     lo = 0
     for size, ahead in zip(CHUNKS, CHUNKS[1:]):
         weigh(lo + size, ahead)
@@ -205,6 +226,7 @@
         lo += size
     angles(0, ua)
     polar(lo, CHUNKS[-1])
+    base[...] = base[...] * MEAN
 
     def pair(j, c):
         angles(2 * j + 1, ub)
@@ -216,7 +238,7 @@
     lax.fori_loop(0, q // 2, pair, 0)
     for h in range(2):
         turned = rows_out[:, h * half : h * half + half].T
-        out[pl.ds(h, half, stride=2), :] = turned[:, :q]
+        out[pl.ds(h, half, stride=2), :] = (turned * unit_of[h * half : h * half + half, :])[:, :q]
 
 
 def partial_ratios(own, mate, coefficients, triples, n, q):
@@ -231,7 +253,7 @@
         out_specs=vmem,
         scratch_shapes=[
             pltpu.VMEM(coefficients.shape, jnp.bfloat16),
-            pltpu.VMEM(triples.shape, jnp.int32),
+            pltpu.VMEM((8, waves), jnp.int32),
             pltpu.VMEM((n, orbitals), jnp.bfloat16),
             pltpu.VMEM((n, orbitals), jnp.bfloat16),
             pltpu.VMEM((n, 128), jnp.bfloat16),
@@ -241,6 +263,8 @@
             pltpu.VMEM((waves, n), jnp.float32),
             pltpu.VMEM((waves, n), jnp.float32),
             pltpu.VMEM((128, n), jnp.float32),
+            pltpu.VMEM((8, n), jnp.float32),
+            pltpu.VMEM((n, 128), jnp.float32),
             pltpu.SemaphoreType.DMA((5,)),
         ],
         compiler_params=pltpu.CompilerParams(vmem_limit_bytes=52 << 20),
@@ -253,15 +277,17 @@
 ):
     q = quad_table.shape[2]
     half = n // 2
-    msg, scale = pack(rotation, assignment, inverse_rows, elec_pos, ion_pos, quad_table, half)
+    msg, kept = pack(
+        rotation, assignment, inverse_rows, elec_pos, ion_pos, quad_table, triples, half
+    )
     sides = [list(range(c, n, 2)) for c in range(2)]
     own = lax.all_to_all(
         msg.reshape(half, 1, 384), AXES, 0, 0, axis_index_groups=sides, tiled=True
     ).reshape(3 * half, 128)
     mate = lax.ppermute(own, AXES, [(i, i ^ 1) for i in range(n)])
-    part = partial_ratios(own, mate, coefficients, triples, n, q)
+    part = partial_ratios(own, mate, coefficients, kept, n, q)
     back = lax.all_to_all(part.reshape(n, 1, q), AXES, 0, 0, tiled=True)
-    return jnp.sum(back * scale[0, 0], axis=0)
+    return jnp.sum(back, axis=0)
 
 
 def solution(mesh):

time: 65.2 us -> 63.7 us (0.977)
  local copies, waits for them, and re-layouts: 0.73 us -> 0 us
    pallas_call x1, Pallas kernels: 10.7 us -> 9.8 us  [partial_ratios(): pl.pallas_call(wave_kernel, out_shape=jax.ShapeDtypeStruct((n, q), jnp.fl...]
    unnamed x4 -> x0, local copies, waits for them, and re-layouts: 0.73 us -> none
where the time goes in v3:
time: 63.7 us; the launch traced here: 63.4 us
  blocking collectives  45.5 us (71%)
  Pallas kernels  11.9 us (19%)
  starting transfers between devices  2.85 us (4%)
  between operations  1.31 us (2%)
  waiting for transfers between devices  1.07 us (2%)
  other arithmetic  0.8 us (1%)
    all_to_all x1, blocking collectives, on_device(): lax.all_to_all(msg.reshape(half, 1, 384), AXES, 0, 0, axis_index_groups=s...  27.4 us
    all_to_all x1, blocking collectives, on_device(): back = lax.all_to_all(part.reshape(n, 1, q), AXES, 0, 0, tiled=True)  18.1 us
    pallas_call x1, Pallas kernels, partial_ratios(): pl.pallas_call(wave_kernel, out_shape=jax.ShapeDtypeStruct((n, q), jnp.fl...  9.8 us
    ppermute x1, starting transfers between devices, on_device(): mate = lax.ppermute(own, AXES, [(i, i ^ 1) for i in range(n)])  2.85 us
    pallas_call x1, Pallas kernels, pack(): pl.pallas_call(pack_kernel, in_specs=[smem, smem, vmem, vmem, vmem, vmem,...  2.12 us
  transfers between devices with their start and end apart: 1, of which 1 were waited for; matrix products, arithmetic and copies ran while one was open for 0% of the time, Pallas kernels for 0%

profile of v3, /device:TPU:1, one launch (start us, length us, event | category | flops | bytes accessed | tf_op | source)
XLA Modules:
  0.0 63.4 jit_solution(8001222969459536227)
XLA Ops:
  1.3 2.1 %pack.1 = (s32[384,128]{1,0:T(8,128)}, s32[640,1152]{1,0:T(8,128)}) custom-call(s32[1]{0:T(128)S(6)} %copy.12.rot, s32[1]{0:T(128)S(6)} %copy.11.asg, f32[1,512]{1,0:T(1,128)} %inv.1, f32[1,3]{1,0:T(1,128)} %bitcast.13, f32[3,128]{1,0:T(4,128)} %ion.1, f32[3,12,64]{2,1,0:T(8,128)} %bitcast.12, s32[3,1152]{1,0:T(4,128)} %triples.1), custom_call_target="tpu_custom_call" | custom-call | tf_op jit(solution)/shard_map/pack/pallas_call | solution.py:73
  3.4 27.4 %all_to_all.10 = s32[128,1,384]{2,1,0:T(1,128)S(1)} all-to-all(s32[128,1,384]{2,1,0:T(1,128)} %bitcast.11), channel_id=1, replica_groups={{0,2,4,6,8,10,12,14,16,18,20,22,24,26,28,30,32,34,36,38,40,42,44,46,48,..., dimensions={0} | all-to-all | bytes 393216 | tf_op jit(solution)/shard_map/all_to_all | solution.py:284
  30.8 2.8 %collective-permute-start = (s32[384,128]{1,0:T(8,128)S(1)}, s32[384,128]{1,0:T(8,128)S(1)}, u32[]{:S(2)}, u32[]{:S(2)}) collective-permute-start(s32[384,128]{1,0:T(8,128)S(1)} %bitcast.8), channel_id=1, source_target_pairs={{0,1},{1,0},{2,3},{3,2},{4,5},{5,4},{6,7},{7,6},{8,9},{9,8},{10,11... | collective-permute-start | bytes 589832 | tf_op jit(solution)/shard_map/ppermute | solution.py:287
  33.7 1.1 %collective-permute-done.mate = s32[384,128]{1,0:T(8,128)S(1)} collective-permute-done((s32[384,128]{1,0:T(8,128)S(1)}, s32[384,128]{1,0:T(8,128)S(1)}, u32[]{:S(2)}, u32[]{:S(2)}) %collective-permute-start) | collective-permute-done | bytes 196640 | tf_op jit(solution)/shard_map/ppermute | solution.py:287
  34.7 9.8 %waves.1 = f32[256,12]{1,0:T(8,128)S(1)} custom-call(s32[384,128]{1,0:T(8,128)S(1)} %bitcast.9, s32[384,128]{1,0:T(8,128)S(1)} %collective-permute-done.mate, bf16[2,1152,512]{2,1,0:T(8,128)(2,1)} %coef_hbm.1, s32[640,1152]{1,0:T(8,128)} %get-tuple-element.8.triples_hbm), custom_call_target="tpu_custom_call" | custom-call | tf_op jit(solution)/shard_map/waves/pallas_call | solution.py:249
  44.5 18.1 %all_to_all.11 = f32[256,1,12]{2,1,0:T(1,128)S(1)} all-to-all(f32[256,1,12]{2,1,0:T(1,128)S(1)} %bitcast.10), channel_id=1, replica_groups=mesh['ga'=4,'orb'=64] {'ga','orb'}, dimensions={0} | all-to-all | bytes 24576 | tf_op jit(solution)/shard_map/all_to_all | solution.py:289
  62.6 0.8 %reduce_sum.11 = f32[12]{0:T(128)} reduce(f32[256,1,12]{2,1,0:T(1,128)S(1)} %all_to_all.11, f32[]{:T(128)} %constant.0.clone.1), dimensions={0,1}, to_apply=%region_0.0 | reduce | flops 3060 | bytes 12340 | tf_op jit(solution)/shard_map/reduce_sum | solution.py:290
Async XLA Ops:
  30.8 3.9 %collective-permute-start = (s32[384,128]{1,0:T(8,128)S(1)}, s32[384,128]{1,0:T(8,128)S(1)}, u32[]{:S(2)}, u32[]{:S(2)}) collective-permute-start(s32[384,128]{1,0:T(8,128)S(1)} %bitcast.8), channel_id=1, source_target_pairs={{0,1},{1,0},{2,3},{3,2},{4,5},{5,4},{6,7},{7,6},{8,9},{9,8},{10,11... | collective-permute-start | bytes 589832 | tf_op jit(solution)/shard_map/ppermute | solution.py:287

commit v4 on v3

--- a/solution.py
+++ b/solution.py
@@ -13,7 +13,9 @@
 CHUNKS = (128, 256, 256, 256, 128, 128)
 C0, C1, C2 = 0.26392367, -1.2978812, 28.72800057
 MEAN = 0.0348596450351644
-T = (0.15911832, 0.02740563, 0.00639816, 0.01881423)
+T = tuple(
+    t * 2.0 ** (0.5 - i) for i, t in enumerate((0.15911832, 0.02740563, 0.00639816, 0.01881423))
+)
 
 
 def pack_kernel(rot, asg, inv, elec, ion, table, triples, msg, kept, eight, sem):
@@ -153,6 +155,7 @@
                 cs, ih[...], NT, preferred_element_type=jnp.float32
             ) + lax.dot_general(cs, il[...], NT, preferred_element_type=jnp.float32)
 
+    copies[0].wait()
     copies[1].wait()
     copies[3].wait()
     weigh(0, first)
@@ -161,7 +164,7 @@
     for h in range(2):
         for r0 in range(0, half, 32):
             word = words(h, r0, 2)
-            scale = jnp.exp2(-word[:, 127:].astype(jnp.float32)) * (1.0 / UP)
+            scale = jnp.exp2(-word[:, 127:].astype(jnp.float32)) * (C2 / UP)
             unit_of[h * half + r0 : h * half + r0 + 32, :] = jnp.broadcast_to(scale, (32, 128))
             high, low = split16(word)
             p1 = (high + 64) >> 7
@@ -170,7 +173,6 @@
             v = jnp.where(lane < w3, p1, jnp.where(lane < 2 * w3, p2, p3))
             parts[h * half + r0 : h * half + r0 + 32, :] = v.astype(jnp.float32).astype(jnp.bfloat16)
     which = (lane[:1] % w3) % q
-    copies[0].wait()
     r = lax.broadcasted_iota(jnp.int32, (8, 128), 1)
     axis = (r % w3) // q
     unit = jnp.where(r < w3, 2.0**-7, jnp.where(r < 2 * w3, 2.0**-14, 2.0**-22))
@@ -184,19 +186,15 @@
         for g in range(lo, lo + count, 16):
             rows = slice(g, g + 16)
             a, b = amp[rows, :], phi[rows, :]
-            aa, ab = jnp.abs(a), jnp.abs(b)
             h = jnp.maximum(a * a + b * b, 1e-36)
             r = lax.rsqrt(h)
-            size = h * r * C2
+            size = h * r
+            x = (b * r) * lax.rsqrt(1.0 + jnp.abs(a) * r)
+            x2 = x * x
+            ang = (((T[3] * x2 + T[2]) * x2 + T[1]) * x2 + T[0]) * x
             amp[rows, :] = size
+            phi[rows, :] = jnp.where(a < 0.0, 0.5 - ang, ang)
             total = total + size[:8] + size[8:]
-            t = jnp.minimum(aa, ab) * r
-            t2 = t * t
-            ang = ((T[3] * t2 + T[2]) * t2 + T[1]) * t2 + T[0]
-            ang = ang * t
-            ang = jnp.where(ab > aa, 0.25 - ang, ang)
-            ang = jnp.where(a < 0.0, 0.5 - ang, ang)
-            phi[rows, :] = jnp.where(b < 0.0, -ang, ang)
         base[...] = total
 
     def angles(k, ref):
@@ -220,22 +218,20 @@
     copies[4].wait()
     base[...] = jnp.zeros_like(base)
     lo = 0
-    for size, ahead in zip(CHUNKS, CHUNKS[1:]):
+    for i, (size, ahead) in enumerate(zip(CHUNKS, CHUNKS[1:])):
         weigh(lo + size, ahead)
+        if i == 2:
+            angles(0, ua)
         polar(lo, size)
         lo += size
-    angles(0, ua)
     polar(lo, CHUNKS[-1])
     base[...] = base[...] * MEAN
 
-    def pair(j, c):
-        angles(2 * j + 1, ub)
-        contract(2 * j, ua)
-        angles(jnp.minimum(2 * j + 2, q - 1), ua)
-        contract(2 * j + 1, ub)
-        return c
-
-    lax.fori_loop(0, q // 2, pair, 0)
+    for k in range(q):
+        held, free = (ua, ub) if k % 2 == 0 else (ub, ua)
+        if k + 1 < q:
+            angles(k + 1, free)
+        contract(k, held)
     for h in range(2):
         turned = rows_out[:, h * half : h * half + half].T
         out[pl.ds(h, half, stride=2), :] = (turned * unit_of[h * half : h * half + half, :])[:, :q]

time: 63.7 us -> 62.3 us (0.978)
  Pallas kernels: 11.9 us -> 10.5 us
    pallas_call x1, Pallas kernels: 9.8 us -> 8.41 us  [partial_ratios(): pl.pallas_call(wave_kernel, out_shape=jax.ShapeDtypeStruct((n, q), jnp.fl...]
where the time goes in v4:
time: 62.3 us; the launch traced here: 62 us
  blocking collectives  45.5 us (73%)
  Pallas kernels  10.5 us (17%)
  starting transfers between devices  2.85 us (5%)
  between operations  1.31 us (2%)
  waiting for transfers between devices  1.07 us (2%)
  other arithmetic  0.8 us (1%)
    all_to_all x1, blocking collectives, on_device(): lax.all_to_all(msg.reshape(half, 1, 384), AXES, 0, 0, axis_index_groups=s...  27.4 us
    all_to_all x1, blocking collectives, on_device(): back = lax.all_to_all(part.reshape(n, 1, q), AXES, 0, 0, tiled=True)  18.1 us
    pallas_call x1, Pallas kernels, partial_ratios(): pl.pallas_call(wave_kernel, out_shape=jax.ShapeDtypeStruct((n, q), jnp.fl...  8.41 us
    ppermute x1, starting transfers between devices, on_device(): mate = lax.ppermute(own, AXES, [(i, i ^ 1) for i in range(n)])  2.85 us
    pallas_call x1, Pallas kernels, pack(): pl.pallas_call(pack_kernel, in_specs=[smem, smem, vmem, vmem, vmem, vmem,...  2.12 us
  transfers between devices with their start and end apart: 1, of which 1 were waited for; matrix products, arithmetic and copies ran while one was open for 0% of the time, Pallas kernels for 0%

profile of v4, /device:TPU:1, one launch (start us, length us, event | category | flops | bytes accessed | tf_op | source)
XLA Modules:
  0.0 62.0 jit_solution(13230776412724020744)
XLA Ops:
  1.3 2.1 %pack.1 = (s32[384,128]{1,0:T(8,128)}, s32[640,1152]{1,0:T(8,128)}) custom-call(s32[1]{0:T(128)S(6)} %copy.12.rot, s32[1]{0:T(128)S(6)} %copy.11.asg, f32[1,512]{1,0:T(1,128)} %inv.1, f32[1,3]{1,0:T(1,128)} %bitcast.13, f32[3,128]{1,0:T(4,128)} %ion.1, f32[3,12,64]{2,1,0:T(8,128)} %bitcast.12, s32[3,1152]{1,0:T(4,128)} %triples.1), custom_call_target="tpu_custom_call" | custom-call | tf_op jit(solution)/shard_map/pack/pallas_call | solution.py:75
  3.4 27.4 %all_to_all.10 = s32[128,1,384]{2,1,0:T(1,128)S(1)} all-to-all(s32[128,1,384]{2,1,0:T(1,128)} %bitcast.11), channel_id=1, replica_groups={{0,2,4,6,8,10,12,14,16,18,20,22,24,26,28,30,32,34,36,38,40,42,44,46,48,..., dimensions={0} | all-to-all | bytes 393216 | tf_op jit(solution)/shard_map/all_to_all | solution.py:280
  30.8 2.8 %collective-permute-start = (s32[384,128]{1,0:T(8,128)S(1)}, s32[384,128]{1,0:T(8,128)S(1)}, u32[]{:S(2)}, u32[]{:S(2)}) collective-permute-start(s32[384,128]{1,0:T(8,128)S(1)} %bitcast.8), channel_id=1, source_target_pairs={{0,1},{1,0},{2,3},{3,2},{4,5},{5,4},{6,7},{7,6},{8,9},{9,8},{10,11... | collective-permute-start | bytes 589832 | tf_op jit(solution)/shard_map/ppermute | solution.py:283
  33.7 1.1 %collective-permute-done.mate = s32[384,128]{1,0:T(8,128)S(1)} collective-permute-done((s32[384,128]{1,0:T(8,128)S(1)}, s32[384,128]{1,0:T(8,128)S(1)}, u32[]{:S(2)}, u32[]{:S(2)}) %collective-permute-start) | collective-permute-done | bytes 196640 | tf_op jit(solution)/shard_map/ppermute | solution.py:283
  34.7 8.4 %waves.1 = f32[256,12]{1,0:T(8,128)S(1)} custom-call(s32[384,128]{1,0:T(8,128)S(1)} %bitcast.9, s32[384,128]{1,0:T(8,128)S(1)} %collective-permute-done.mate, bf16[2,1152,512]{2,1,0:T(8,128)(2,1)} %coef_hbm.1, s32[640,1152]{1,0:T(8,128)} %get-tuple-element.8.triples_hbm), custom_call_target="tpu_custom_call" | custom-call | tf_op jit(solution)/shard_map/waves/pallas_call | solution.py:245
  43.2 18.1 %all_to_all.11 = f32[256,1,12]{2,1,0:T(1,128)S(1)} all-to-all(f32[256,1,12]{2,1,0:T(1,128)S(1)} %bitcast.10), channel_id=1, replica_groups=mesh['ga'=4,'orb'=64] {'ga','orb'}, dimensions={0} | all-to-all | bytes 24576 | tf_op jit(solution)/shard_map/all_to_all | solution.py:285
  61.3 0.8 %reduce_sum.11 = f32[12]{0:T(128)} reduce(f32[256,1,12]{2,1,0:T(1,128)S(1)} %all_to_all.11, f32[]{:T(128)} %constant.0.clone.1), dimensions={0,1}, to_apply=%region_0.0 | reduce | flops 3060 | bytes 12340 | tf_op jit(solution)/shard_map/reduce_sum | solution.py:286
Async XLA Ops:
  30.8 3.9 %collective-permute-start = (s32[384,128]{1,0:T(8,128)S(1)}, s32[384,128]{1,0:T(8,128)S(1)}, u32[]{:S(2)}, u32[]{:S(2)}) collective-permute-start(s32[384,128]{1,0:T(8,128)S(1)} %bitcast.8), channel_id=1, source_target_pairs={{0,1},{1,0},{2,3},{3,2},{4,5},{5,4},{6,7},{7,6},{8,9},{9,8},{10,11... | collective-permute-start | bytes 589832 | tf_op jit(solution)/shard_map/ppermute | solution.py:283

commit v5 on v4

--- a/solution.py
+++ b/solution.py
@@ -10,7 +10,7 @@
 AXES = ("ga", "orb")
 UP = 2.0**40
 KEPT_ROWS = 640
-CHUNKS = (128, 256, 256, 256, 128, 128)
+CHUNKS = (128, 256, 256, 256, 256)
 C0, C1, C2 = 0.26392367, -1.2978812, 28.72800057
 MEAN = 0.0348596450351644
 T = tuple(

time: 62.3 us -> 62.1 us (level)
  no operation moved by 1% of the time
where the time goes in v5:
time: 62.1 us; the launch traced here: 61.8 us
  blocking collectives  45.5 us (73%)
  Pallas kernels  10.3 us (17%)
  starting transfers between devices  2.85 us (5%)
  between operations  1.31 us (2%)
  waiting for transfers between devices  1.07 us (2%)
  other arithmetic  0.8 us (1%)
    all_to_all x1, blocking collectives, on_device(): lax.all_to_all(msg.reshape(half, 1, 384), AXES, 0, 0, axis_index_groups=s...  27.4 us
    all_to_all x1, blocking collectives, on_device(): back = lax.all_to_all(part.reshape(n, 1, q), AXES, 0, 0, tiled=True)  18.1 us
    pallas_call x1, Pallas kernels, partial_ratios(): pl.pallas_call(wave_kernel, out_shape=jax.ShapeDtypeStruct((n, q), jnp.fl...  8.19 us
    ppermute x1, starting transfers between devices, on_device(): mate = lax.ppermute(own, AXES, [(i, i ^ 1) for i in range(n)])  2.85 us
    pallas_call x1, Pallas kernels, pack(): pl.pallas_call(pack_kernel, in_specs=[smem, smem, vmem, vmem, vmem, vmem,...  2.12 us
  transfers between devices with their start and end apart: 1, of which 1 were waited for; matrix products, arithmetic and copies ran while one was open for 0% of the time, Pallas kernels for 0%

profile of v5, /device:TPU:1, one launch (start us, length us, event | category | flops | bytes accessed | tf_op | source)
XLA Modules:
  0.0 61.8 jit_solution(14799312957023118667)
XLA Ops:
  1.3 2.1 %pack.1 = (s32[384,128]{1,0:T(8,128)}, s32[640,1152]{1,0:T(8,128)}) custom-call(s32[1]{0:T(128)S(6)} %copy.12.rot, s32[1]{0:T(128)S(6)} %copy.11.asg, f32[1,512]{1,0:T(1,128)} %inv.1, f32[1,3]{1,0:T(1,128)} %bitcast.13, f32[3,128]{1,0:T(4,128)} %ion.1, f32[3,12,64]{2,1,0:T(8,128)} %bitcast.12, s32[3,1152]{1,0:T(4,128)} %triples.1), custom_call_target="tpu_custom_call" | custom-call | tf_op jit(solution)/shard_map/pack/pallas_call | solution.py:75
  3.4 27.4 %all_to_all.10 = s32[128,1,384]{2,1,0:T(1,128)S(1)} all-to-all(s32[128,1,384]{2,1,0:T(1,128)} %bitcast.11), channel_id=1, replica_groups={{0,2,4,6,8,10,12,14,16,18,20,22,24,26,28,30,32,34,36,38,40,42,44,46,48,..., dimensions={0} | all-to-all | bytes 393216 | tf_op jit(solution)/shard_map/all_to_all | solution.py:280
  30.8 2.8 %collective-permute-start = (s32[384,128]{1,0:T(8,128)S(1)}, s32[384,128]{1,0:T(8,128)S(1)}, u32[]{:S(2)}, u32[]{:S(2)}) collective-permute-start(s32[384,128]{1,0:T(8,128)S(1)} %bitcast.8), channel_id=1, source_target_pairs={{0,1},{1,0},{2,3},{3,2},{4,5},{5,4},{6,7},{7,6},{8,9},{9,8},{10,11... | collective-permute-start | bytes 589832 | tf_op jit(solution)/shard_map/ppermute | solution.py:283
  33.7 1.1 %collective-permute-done.mate = s32[384,128]{1,0:T(8,128)S(1)} collective-permute-done((s32[384,128]{1,0:T(8,128)S(1)}, s32[384,128]{1,0:T(8,128)S(1)}, u32[]{:S(2)}, u32[]{:S(2)}) %collective-permute-start) | collective-permute-done | bytes 196640 | tf_op jit(solution)/shard_map/ppermute | solution.py:283
  34.7 8.2 %waves.1 = f32[256,12]{1,0:T(8,128)S(1)} custom-call(s32[384,128]{1,0:T(8,128)S(1)} %bitcast.9, s32[384,128]{1,0:T(8,128)S(1)} %collective-permute-done.mate, bf16[2,1152,512]{2,1,0:T(8,128)(2,1)} %coef_hbm.1, s32[640,1152]{1,0:T(8,128)} %get-tuple-element.8.triples_hbm), custom_call_target="tpu_custom_call" | custom-call | tf_op jit(solution)/shard_map/waves/pallas_call | solution.py:245
  42.9 18.1 %all_to_all.11 = f32[256,1,12]{2,1,0:T(1,128)S(1)} all-to-all(f32[256,1,12]{2,1,0:T(1,128)S(1)} %bitcast.10), channel_id=1, replica_groups=mesh['ga'=4,'orb'=64] {'ga','orb'}, dimensions={0} | all-to-all | bytes 24576 | tf_op jit(solution)/shard_map/all_to_all | solution.py:285
  61.0 0.8 %reduce_sum.11 = f32[12]{0:T(128)} reduce(f32[256,1,12]{2,1,0:T(1,128)S(1)} %all_to_all.11, f32[]{:T(128)} %constant.0.clone.1), dimensions={0,1}, to_apply=%region_0.0 | reduce | flops 3060 | bytes 12340 | tf_op jit(solution)/shard_map/reduce_sum | solution.py:286
Async XLA Ops:
  30.8 3.9 %collective-permute-start = (s32[384,128]{1,0:T(8,128)S(1)}, s32[384,128]{1,0:T(8,128)S(1)}, u32[]{:S(2)}, u32[]{:S(2)}) collective-permute-start(s32[384,128]{1,0:T(8,128)S(1)} %bitcast.8), channel_id=1, source_target_pairs={{0,1},{1,0},{2,3},{3,2},{4,5},{5,4},{6,7},{7,6},{8,9},{9,8},{10,11... | collective-permute-start | bytes 589832 | tf_op jit(solution)/shard_map/ppermute | solution.py:283

commit v6 on v5

--- a/solution.py
+++ b/solution.py
@@ -18,7 +18,7 @@
 )
 
 
-def pack_kernel(rot, asg, inv, elec, ion, table, triples, msg, kept, eight, sem):
+def pack_kernel(rot, asg, inv, elec, ion, table, triples, msg, kept, eight, block, sem, sends_sem):
     eight[...] = jnp.zeros_like(eight)
     eight[0:3, :] = triples[...]
     keep = pltpu.make_async_copy(eight, kept.at[pl.ds(0, 8), :], sem)
@@ -64,8 +64,15 @@
         jnp.broadcast_to(words[:, :128], (24, 128)),
         jnp.where(r == 1, jnp.broadcast_to(words[:, 128:], (24, 128)), coords),
     )
-    for i in range(msg.shape[0] // 24):
-        msg[pl.ds(24 * i, 24), :] = tile
+    block[...] = tile
+    sends = [
+        pltpu.make_async_copy(block, msg.at[pl.ds(24 * i, 24), :], sends_sem.at[i])
+        for i in range(msg.shape[0] // 24)
+    ]
+    for send in sends:
+        send.start()
+    for send in sends:
+        send.wait()
     keep.wait()
 
 
@@ -75,14 +82,16 @@
     return pl.pallas_call(
         pack_kernel,
         in_specs=[smem, smem, vmem, vmem, vmem, vmem, vmem],
-        out_specs=[vmem, pl.BlockSpec(memory_space=pltpu.HBM)],
+        out_specs=[pl.BlockSpec(memory_space=pltpu.HBM)] * 2,
         out_shape=[
             jax.ShapeDtypeStruct((3 * n, 128), jnp.int32),
             jax.ShapeDtypeStruct((KEPT_ROWS, triples.shape[1]), jnp.int32),
         ],
         scratch_shapes=[
             pltpu.VMEM((8, triples.shape[1]), jnp.int32),
+            pltpu.VMEM((24, 128), jnp.int32),
             pltpu.SemaphoreType.DMA,
+            pltpu.SemaphoreType.DMA((n // 8,)),
         ],
         name="pack",
     )(

time: 62.1 us -> 62 us (level)
  no operation moved by 1% of the time
where the time goes in v6:
time: 62 us; the launch traced here: 61.7 us
  blocking collectives  45.5 us (73%)
  Pallas kernels  10.2 us (16%)
  starting transfers between devices  2.85 us (5%)
  between operations  1.31 us (2%)
  waiting for transfers between devices  1.07 us (2%)
  other arithmetic  0.8 us (1%)
    all_to_all x1, blocking collectives, on_device(): lax.all_to_all(msg.reshape(half, 1, 384), AXES, 0, 0, axis_index_groups=s...  27.4 us
    all_to_all x1, blocking collectives, on_device(): back = lax.all_to_all(part.reshape(n, 1, q), AXES, 0, 0, tiled=True)  18.1 us
    pallas_call x1, Pallas kernels, partial_ratios(): pl.pallas_call(wave_kernel, out_shape=jax.ShapeDtypeStruct((n, q), jnp.fl...  8.2 us
    ppermute x1, starting transfers between devices, on_device(): mate = lax.ppermute(own, AXES, [(i, i ^ 1) for i in range(n)])  2.85 us
    pallas_call x1, Pallas kernels, pack(): pl.pallas_call(pack_kernel, in_specs=[smem, smem, vmem, vmem, vmem, vmem,...  1.98 us
  transfers between devices with their start and end apart: 1, of which 1 were waited for; matrix products, arithmetic and copies ran while one was open for 0% of the time, Pallas kernels for 0%

profile of v6, /device:TPU:1, one launch (start us, length us, event | category | flops | bytes accessed | tf_op | source)
XLA Modules:
  0.0 61.7 jit_solution(8987900653690454848)
XLA Ops:
  1.3 2.0 %pack.1 = (s32[384,128]{1,0:T(8,128)}, s32[640,1152]{1,0:T(8,128)}) custom-call(s32[1]{0:T(128)S(6)} %copy.12.rot, s32[1]{0:T(128)S(6)} %copy.11.asg, f32[1,512]{1,0:T(1,128)} %inv.1, f32[1,3]{1,0:T(1,128)} %bitcast.13, f32[3,128]{1,0:T(4,128)} %ion.1, f32[3,12,64]{2,1,0:T(8,128)} %bitcast.12, s32[3,1152]{1,0:T(4,128)} %triples.1), custom_call_target="tpu_custom_call" | custom-call | tf_op jit(solution)/shard_map/pack/pallas_call | solution.py:82
  3.3 27.4 %all_to_all.10 = s32[128,1,384]{2,1,0:T(1,128)S(1)} all-to-all(s32[128,1,384]{2,1,0:T(1,128)} %bitcast.11), channel_id=1, replica_groups={{0,2,4,6,8,10,12,14,16,18,20,22,24,26,28,30,32,34,36,38,40,42,44,46,48,..., dimensions={0} | all-to-all | bytes 393216 | tf_op jit(solution)/shard_map/all_to_all | solution.py:289
  30.7 2.8 %collective-permute-start = (s32[384,128]{1,0:T(8,128)S(1)}, s32[384,128]{1,0:T(8,128)S(1)}, u32[]{:S(2)}, u32[]{:S(2)}) collective-permute-start(s32[384,128]{1,0:T(8,128)S(1)} %bitcast.8), channel_id=1, source_target_pairs={{0,1},{1,0},{2,3},{3,2},{4,5},{5,4},{6,7},{7,6},{8,9},{9,8},{10,11... | collective-permute-start | bytes 589832 | tf_op jit(solution)/shard_map/ppermute | solution.py:292
  33.5 1.1 %collective-permute-done.mate = s32[384,128]{1,0:T(8,128)S(1)} collective-permute-done((s32[384,128]{1,0:T(8,128)S(1)}, s32[384,128]{1,0:T(8,128)S(1)}, u32[]{:S(2)}, u32[]{:S(2)}) %collective-permute-start) | collective-permute-done | bytes 196640 | tf_op jit(solution)/shard_map/ppermute | solution.py:292
  34.6 8.2 %waves.1 = f32[256,12]{1,0:T(8,128)S(1)} custom-call(s32[384,128]{1,0:T(8,128)S(1)} %bitcast.9, s32[384,128]{1,0:T(8,128)S(1)} %collective-permute-done.mate, bf16[2,1152,512]{2,1,0:T(8,128)(2,1)} %coef_hbm.1, s32[640,1152]{1,0:T(8,128)} %get-tuple-element.8.triples_hbm), custom_call_target="tpu_custom_call" | custom-call | tf_op jit(solution)/shard_map/waves/pallas_call | solution.py:254
  42.8 18.1 %all_to_all.11 = f32[256,1,12]{2,1,0:T(1,128)S(1)} all-to-all(f32[256,1,12]{2,1,0:T(1,128)S(1)} %bitcast.10), channel_id=1, replica_groups=mesh['ga'=4,'orb'=64] {'ga','orb'}, dimensions={0} | all-to-all | bytes 24576 | tf_op jit(solution)/shard_map/all_to_all | solution.py:294
  60.9 0.8 %reduce_sum.11 = f32[12]{0:T(128)} reduce(f32[256,1,12]{2,1,0:T(1,128)S(1)} %all_to_all.11, f32[]{:T(128)} %constant.0.clone.1), dimensions={0,1}, to_apply=%region_0.0 | reduce | flops 3060 | bytes 12340 | tf_op jit(solution)/shard_map/reduce_sum | solution.py:295
Async XLA Ops:
  30.7 3.9 %collective-permute-start = (s32[384,128]{1,0:T(8,128)S(1)}, s32[384,128]{1,0:T(8,128)S(1)}, u32[]{:S(2)}, u32[]{:S(2)}) collective-permute-start(s32[384,128]{1,0:T(8,128)S(1)} %bitcast.8), channel_id=1, source_target_pairs={{0,1},{1,0},{2,3},{3,2},{4,5},{5,4},{6,7},{7,6},{8,9},{9,8},{10,11... | collective-permute-start | bytes 589832 | tf_op jit(solution)/shard_map/ppermute | solution.py:292
